TPU v7x, 128 devices: a whole 4x4x4 slice. The times are simulated.
128 devices in a mesh: tm: 64 (over z_hi, x, y, core), inp: 2 (over z_lo).
Axes of the slice: x: 4, y: 4, z: 4 (z_hi: 2, z_lo: 2; z = z_hi * 2 + z_lo), core: 2. Of those that a mesh axis runs over, the one named last changes fastest.
Arguments:
- voltages: bfloat16 [2, 262144, 1024], P(None, 'tm', 'inp'), may hold values from -127 to 127, as said below
- taps: int32 [12, 1024], replicated, may hold values from -64 to 64
Outputs:
- visibility: bfloat16 [512, 1024, 1024], P(('tm', 'inp'))
Inputs may be any that keep to these rules, and one draw needn't show every extreme that they name: `voltages`: every sample is a whole number.
All inputs are finite; a program needn't handle non-finite values.
Results may differ from a plain program's by a relative error of at most 0.0048.
Values may be sent and summed in bfloat16 or wider, within the bound.
A program may use at most 576 MiB of HBM per device.

v0:
```python
import math

import jax
import jax.numpy as jnp
from jax import lax
from jax.sharding import PartitionSpec as P

KEEP = 512


def passed_along(value, axis, steps):
    count = lax.axis_size(axis)
    first, last = (max(0, -steps), min(count, count - steps))
    return lax.ppermute(value, axis, [(source, source + steps) for source in range(first, last)])


def dft_table(fine_count, keep_count):
    branch = jnp.arange(fine_count, dtype=jnp.int32)[:, None]
    channel = jnp.arange(keep_count, dtype=jnp.int32)[None, :] - keep_count // 2
    phase_index = jnp.mod(branch * channel, fine_count).astype(jnp.float32)
    angles = 2.0 * math.pi / fine_count * phase_index
    norm_scale = 1.0 / math.sqrt(fine_count)
    cosine = jnp.cos(angles) * norm_scale
    sine_part = jnp.sin(angles) * norm_scale
    dft_matrix = jnp.stack(
        [jnp.stack([cosine, -sine_part], 1), jnp.stack([sine_part, cosine], 1)], 0
    )
    return dft_matrix.astype(jnp.bfloat16)


def finish(products, chan_count, all_inputs, spec_total):
    visibility = products.reshape(chan_count, 2, all_inputs, all_inputs) * (1.0 / spec_total)
    upper_mask = jnp.arange(all_inputs)[:, None] <= jnp.arange(all_inputs)[None, :]
    return jnp.where(upper_mask[None], visibility[:, 0], visibility[:, 1]).astype(jnp.bfloat16)


def per_device(voltages, taps):
    history_len = taps.shape[0] - 1
    fine_count = taps.shape[1]
    frames = voltages.shape[1] // fine_count
    input_width = voltages.shape[2]
    keep_count = KEEP
    coefficient = taps.astype(jnp.float32)
    dft_matrix = dft_table(fine_count, keep_count)
    n_time = lax.axis_size("tm")
    n_group = lax.axis_size("inp")
    chan_count = keep_count // (n_time * n_group)
    all_inputs = n_group * input_width
    spec_total = n_time * frames
    own_frames = voltages.reshape(2, frames, fine_count, input_width)
    pieces = [own_frames]
    remaining = history_len
    shift_count = (history_len + frames - 1) // frames
    for offset in range(1, shift_count + 1):
        take_count = min(remaining, frames)
        received = passed_along(own_frames[:, frames - take_count :], "tm", offset)
        pieces.insert(0, received)
        remaining = remaining - take_count
    extended = jnp.concatenate(pieces, axis=1)
    filtered = coefficient[0][None, None, :, None] * extended[
        :, history_len : history_len + frames
    ].astype(jnp.float32)
    for k in range(1, history_len + 1):
        filtered = filtered + coefficient[k][None, None, :, None] * extended[
            :, history_len - k : history_len - k + frames
        ].astype(jnp.float32)
    filtered = (filtered * (1.0 / 8192.0)).astype(jnp.bfloat16)
    spectra = jnp.einsum(
        "rfna,rnsj->jsfa", filtered, dft_matrix, preferred_element_type=jnp.float32
    ).astype(jnp.bfloat16)
    flat_spectra = spectra.reshape(keep_count, 2, frames * input_width)
    exchanged = lax.all_to_all(flat_spectra, ("tm", "inp"), split_axis=0, concat_axis=2, tiled=True)
    channel_grid = exchanged.reshape(chan_count, 2, n_time, n_group, frames, input_width)
    einsum_form = "crtgfa,csrthfb->csgahb"
    rotated = jnp.stack([-channel_grid[:, 1], channel_grid[:, 0]], axis=1)
    turned = jnp.stack([channel_grid, rotated], axis=1)
    products = jnp.einsum(einsum_form, channel_grid, turned, preferred_element_type=jnp.float32)
    return finish(products, chan_count, all_inputs, spec_total)


def solution(mesh):
    placed = (P(None, "tm", "inp"), P())
    return jax.shard_map(
        per_device,
        mesh=mesh,
        in_specs=placed,
        out_specs=P(("tm", "inp"), None, None),
        check_vma=False,
    )
```

profile of v0, /device:TPU:1, one launch (start us, length us, event | category | flops | bytes accessed | tf_op | source)
XLA Modules:
  0.0 758.6 jit_solution(5823844590932739800)
XLA Ops:
  0.0 11.4 %copy.11 = bf16[2,4,1024,512]{2,3,0,1:T(8,128)(2,1)} copy(bf16[2,4,1024,512]{3,2,1,0:T(8,128)(2,1)} %bitcast.81) | data formatting | bytes 16777216 | tf_op jit(solution)/shard_map/reshape | solution.py:50
  11.4 4.7 collective-permute-start.1
  16.0 3.5 collective-permute-start
  19.6 6.8 slice.130
  26.4 5.9 collective-permute-start.2
  32.3 8.8 %negate_convert_fusion = (bf16[1024,1,512]{2,0,1:T(8,128)(2,1)S(1)}, bf16[1024,1,512]{2,0,1:T(8,128)(2,1)S(1)}, bf16[1024,1,512]{2,0,1:T(8,128)(2,1)S(1)}) fusion(s32[512]{0:T(512)S(1)} %iota_add_fusion), kind=kLoop, calls=%fused_computation.35 | loop fusion | flops 10485760 | bytes 3147776 | tf_op jit(solution)/shard_map/convert.7
  42.9 377.9 %collective-permute-done.2 = bf16[2,3,1024,512]{2,3,0,1:T(8,128)(2,1)} collective-permute-done((bf16[2,3,1024,512]{2,3,0,1:T(8,128)(2,1)}, bf16[2,3,1024,512]{2,3,0,1:T(8,128)(2,1)}, u32[]{:S(2)}, u32[]{:S(2)}) %collective-permute-start.2) | collective-permute-done | bytes 6291488 | tf_op jit(solution)/shard_map/ppermute | solution.py:14
  420.8 6.8 constant_dynamic-update-slice_fusion.3
  427.6 7.4 constant_dynamic-update-slice_fusion.1
  436.0 3.3 copy-done.2
  439.3 7.6 %constant_dynamic-update-slice_fusion = bf16[2,8,1024,512]{2,3,0,1:T(8,128)(2,1)} fusion(bf16[2,8,1024,512]{2,3,0,1:T(8,128)(2,1)} %get-tuple-element.5, bf16[2,4,1024,512]{2,3,0,1:T(8,128)(2,1)} %copy-done.2), kind=kLoop, calls=%fused_computation.42 | loop fusion | bytes 16777216 | tf_op jit(solution)/shard_map/concatenate | solution.py:59
  446.9 38.9 %bitcast_convert_fusion = bf16[2,512,4,512]{1,3,2,0:T(8,128)(2,1)} fusion(bf16[2,7,1024,512]{2,3,0,1:T(8,128)(2,1)} %get-tuple-element.6, f32[1024]{0:T(1024)S(1)} %bitcast.84, f32[1024]{0:T(1024)S(1)} %bitcast.85, f32[1024]{0:T(1024)S(1)} %bitcast.86, bf16[2,4,1024,512]{2,3,0,1:T(8,128)(2,1)} %copy-done.1, f32[1024]{0:T(1024)S(1)} %bitcast.87, ...), kind=kOutput, calls=%fused_computation.17 | convolution fusion | flops 8793358336 | bytes 83935232 | tf_op jit(solution)/shard_map/rfna,rnsj->jsfa/dot_general | solution.py:68
  485.8 11.3 %copy.16 = bf16[512,2,2048]{2,1,0:T(2,128)(2,1)} copy(bf16[512,2,2048]{0,2,1:T(8,128)(2,1)} %bitcast.82) | data formatting | bytes 8388608 | tf_op jit(solution)/shard_map/reshape | solution.py:71
  497.1 80.0 %all-to-all-start = ((bf16[512,2,2048]{2,1,0:T(2,128)(2,1)}), bf16[512,2,2048]{2,1,0:T(2,128)(2,1)}, u32[]{:S(2)}, u32[]{:S(2)}) async-start(bf16[512,2,2048]{2,1,0:T(2,128)(2,1)} %copy.16), calls=%async_computation | async-start | bytes 8388608 | tf_op jit(solution)/shard_map/all_to_all | solution.py:72
  577.3 53.5 %all-to-all-done = bf16[512,2,2048]{2,1,0:T(2,128)(2,1)} async-done(((bf16[512,2,2048]{2,1,0:T(2,128)(2,1)}), bf16[512,2,2048]{2,1,0:T(2,128)(2,1)}, u32[]{:S(2)}, u32[]{:S(2)}) %all-to-all-start) | async-done | bytes 4194336 | tf_op jit(solution)/shard_map/all_to_all | solution.py:72
  630.8 7.6 reshape.176
  638.4 7.6 %reshape.175 = bf16[4,1,2,64,2,4,512]{6,5,2,0,4,3,1:T(4,128)(2,1)} reshape(bf16[4,2,128,2048]{3,1,0,2:T(2,128)(2,1)} %bitcast.24) | data formatting | bytes 8388608 | tf_op jit(solution)/shard_map/stack;reshape | solution.py:76
  646.0 3.7 fusion.24
  650.9 2.4 copy_negate_fusion
  653.4 4.4 copy.21
  660.1 20.4 %fusion = bf16[4,2,2,512,2,512]{3,5,2,4,1,0:T(8,128)(2,1)} fusion(bf16[4,1,2,64,2,4,512]{6,3,2,5,4,1,0:T(8,128)(2,1)} %maximum_bitcast_fusion.4, bf16[4,1,2,64,2,4,512]{6,3,2,5,4,1,0:T(8,128)(2,1)} %copy.21, bf16[4,2,64,2,4,512,1,1]{5,4,1,0,3,2,7,6:T(4,128)(2,1)} %bitcast.80), kind=kOutput, calls=%fused_computation.1 | convolution fusion | flops 8623489024 | bytes 29360128 | tf_op jit(solution)/shard_map/crtgfa,csrthfb->csgahb/dot_general | solution.py:77
  680.5 41.5 %copy.23 = bf16[4,2,2,512,2,512]{5,4,3,2,1,0:T(2,128)(2,1)} copy(bf16[4,2,2,512,2,512]{3,5,2,4,1,0:T(8,128)(2,1)} %fusion) | data formatting | bytes 33554432 | tf_op jit(solution)/shard_map/mul | solution.py:32
  722.0 27.3 %mul.287 = bf16[4,2,1024,1024]{3,2,1,0:T(8,128)(2,1)} reshape(bf16[4,2,2,512,2,512]{5,4,3,2,1,0:T(2,128)(2,1)} %copy.23) | data formatting | bytes 33554432 | tf_op jit(solution)/shard_map/mul | solution.py:32
  749.3 9.3 %fusion.2 = bf16[4,1024,1024]{2,1,0:T(8,128)(2,1)} fusion(bf16[4,2,1024,1024]{3,2,1,0:T(8,128)(2,1)} %mul.287, pred[1024,1024]{1,0:T(8,128)(4,1)S(1)} %iota_compare_fusion), kind=kLoop, calls=%fused_computation.8 | loop fusion | flops 4194304 | bytes 26214400 | tf_op jit(solution)/shard_map/convert_element_type | solution.py:34
  (16 shorter events, 6.5 us)
Async XLA Ops:
  11.4 20.9 %copy-start.3 = (s32[12,1024]{1,0:T(8,128)S(1)}, s32[12,1024]{1,0:T(8,128)}, u32[]{:S(2)}) copy-start(s32[12,1024]{1,0:T(8,128)} %param.3) | copy-start | bytes 147460
  11.4 416.3 %collective-permute-start.1 = (bf16[2,4,1024,512]{2,3,0,1:T(8,128)(2,1)}, bf16[2,4,1024,512]{2,3,0,1:T(8,128)(2,1)S(1)}, u32[]{:S(2)}, u32[]{:S(2)}) collective-permute-start(bf16[2,4,1024,512]{2,3,0,1:T(8,128)(2,1)} %copy.11), channel_id=1, source_target_pairs={{0,4},{2,6},{4,8},{6,10},{8,12},{10,14},{12,16},{14,18},{16,20},{1... | collective-permute-start | bytes 25165832 | tf_op jit(solution)/shard_map/ppermute | solution.py:14
  16.0 420.0 %collective-permute-start = (bf16[2,4,1024,512]{2,3,0,1:T(8,128)(2,1)}, bf16[2,4,1024,512]{2,3,0,1:T(8,128)(2,1)S(1)}, u32[]{:S(2)}, u32[]{:S(2)}) collective-permute-start(bf16[2,4,1024,512]{2,3,0,1:T(8,128)(2,1)} %copy.11), channel_id=1, source_target_pairs={{0,2},{2,4},{4,6},{6,8},{8,10},{10,12},{12,14},{14,16},{16,18},{18... | collective-permute-start | bytes 25165832 | tf_op jit(solution)/shard_map/ppermute | solution.py:14
  26.4 394.4 %collective-permute-start.2 = (bf16[2,3,1024,512]{2,3,0,1:T(8,128)(2,1)}, bf16[2,3,1024,512]{2,3,0,1:T(8,128)(2,1)}, u32[]{:S(2)}, u32[]{:S(2)}) collective-permute-start(bf16[2,3,1024,512]{2,3,0,1:T(8,128)(2,1)} %slice.130), channel_id=1, source_target_pairs={{0,6},{2,8},{4,10},{6,12},{8,14},{10,16},{12,18},{14,20},{16,22},{... | collective-permute-start | bytes 18874376 | tf_op jit(solution)/shard_map/ppermute | solution.py:14
  427.6 8.3 %copy-start.1 = (bf16[2,4,1024,512]{2,3,0,1:T(8,128)(2,1)}, bf16[2,4,1024,512]{2,3,0,1:T(8,128)(2,1)S(1)}, u32[]{:S(2)}) copy-start(bf16[2,4,1024,512]{2,3,0,1:T(8,128)(2,1)S(1)} %collective-permute-done.1) | copy-start | bytes 25165828
  436.0 3.3 copy-start.2
  497.1 133.7 %all-to-all-start = ((bf16[512,2,2048]{2,1,0:T(2,128)(2,1)}), bf16[512,2,2048]{2,1,0:T(2,128)(2,1)}, u32[]{:S(2)}, u32[]{:S(2)}) async-start(bf16[512,2,2048]{2,1,0:T(2,128)(2,1)} %copy.16), calls=%async_computation | async-start | bytes 8388608 | tf_op jit(solution)/shard_map/all_to_all | solution.py:72
  646.0 7.4 copy-start
where the time goes:
time: 762 us; the launch traced here: 759 us
  waiting for transfers between devices  431 us (57%)
  local copies, waits for them, and re-layouts  149 us (20%)
  starting transfers between devices  94 us (12%)
  matrix products  59.3 us (8%)
  other arithmetic  24.9 us (3%)
    ppermute x3, waiting for transfers between devices, passed_along(): lax.ppermute(value, axis, [(source, source + steps) for source in range(f...  378 us
    all_to_all x1, starting transfers between devices, per_device(): lax.all_to_all(flat_spectra, ('tm', 'inp'), split_axis=0, concat_axis=2,...  80 us
    mul x2, local copies, waits for them, and re-layouts, finish(): products.reshape(chan_count, 2, all_inputs, all_inputs) * (1.0 / spec_total)  68.8 us
    all_to_all x1, waiting for transfers between devices, per_device(): lax.all_to_all(flat_spectra, ('tm', 'inp'), split_axis=0, concat_axis=2,...  53.5 us
    dot_general x1, matrix products, per_device(): jnp.einsum('rfna,rnsj->jsfa', filtered, dft_matrix, preferred_element_typ...  38.9 us
    dot_general x1, matrix products, per_device(): jnp.einsum(einsum_form, channel_grid, turned, preferred_element_type=jnp....  20.4 us
    unnamed x11, local copies, waits for them, and re-layouts  19.7 us
  transfers between devices with their start and end apart: 4, of which 2 were waited for; matrix products, arithmetic and copies ran while one was open for 4% of the time, Pallas kernels for 0%

commit v1 on v0

v1 whole, which is shorter than its diff:
```python
import functools
import math

import jax
import jax.numpy as jnp
import numpy as np
from jax import lax
from jax.experimental import pallas as pl
from jax.experimental.pallas import tpu as pltpu
from jax.sharding import PartitionSpec as P

KEEP = 512
MESH = pl.DeviceIdType.MESH


def table_parts(fine, keep):
    chan = np.repeat(np.arange(keep) - keep // 2, 2)
    part = np.tile(np.arange(2), keep)
    low = (chan[:, None] * np.arange(128)[None, :] + part[:, None] * (fine // 4)) % fine
    high = (chan[:, None] * np.arange(0, fine, 128)[None, :]) % fine
    scale = 1.0 / math.sqrt(fine)
    step = 2.0 * np.pi / fine
    return tuple(
        x.astype(np.float32)
        for x in (np.cos(step * low) * scale, np.sin(step * low) * scale, np.cos(step * high), np.sin(step * high))
    )


def dft_rows(fine, keep):
    low_cos, low_sin, high_cos, high_sin = (jnp.asarray(x) for x in table_parts(fine, keep))
    first = high_cos[:, :, None] * low_cos[:, None, :] - high_sin[:, :, None] * low_sin[:, None, :]
    second = high_sin[:, :, None] * low_cos[:, None, :] + high_cos[:, :, None] * low_sin[:, None, :]
    rows = first.shape[0]
    both = jnp.stack([first, second], axis=1)
    return both.reshape(rows, 2 * fine).astype(jnp.bfloat16)


def partial_spectra(frames, fine, history, volt, taps, table, out, samples, filtered, stage, wide_taps, in_sem, send_sem, recv_sem, out_sem):
    me = lax.axis_index("tm")
    core = lax.rem(me, 2)
    other = 1 - core
    partner = me + 1 - 2 * core
    span = 2 * frames
    produced = span + history
    half = samples.shape[3]
    barrier = pltpu.get_barrier_semaphore()
    pl.semaphore_signal(barrier, inc=1, device_id={"tm": partner}, device_id_type=MESH)
    pl.semaphore_wait(barrier, 1)

    def lanes(which):
        return pl.ds(pl.multiple_of(which * half, half), half)

    remote = []
    local = []
    for r in range(2):
        for f in range(frames):
            source = volt.at[r, pl.ds(f * fine, fine)]
            remote.append(
                pltpu.make_async_remote_copy(
                    src_ref=source.at[:, lanes(other)],
                    dst_ref=samples.at[core * frames + f, r],
                    send_sem=send_sem.at[r, f],
                    recv_sem=recv_sem.at[r, f],
                    device_id={"tm": partner},
                    device_id_type=MESH,
                )
            )
            local.append(
                pltpu.make_async_copy(source.at[:, lanes(core)], samples.at[core * frames + f, r], in_sem.at[r, f])
            )
    for copy in remote + local:
        copy.start()
    for copy in local + remote:
        copy.wait()

    rows = 16

    @pl.loop(0, fine // rows)
    def _(step):
        at = pl.ds(pl.multiple_of(step * rows, rows), rows)
        tap_rows = taps[at, :]
        for k in range(history + 1):
            wide_taps[k] = jnp.broadcast_to(tap_rows[:, k : k + 1], (rows, 128))
        for r in range(2):
            for lane in range(half // 128):
                cols = pl.ds(lane * 128, 128)
                held = [samples[i, r, at, cols].astype(jnp.float32) for i in range(span)]
                for f in range(produced):
                    total = None
                    for i in range(span):
                        if 0 <= f - i <= history:
                            term = wide_taps[f - i] * held[i]
                            total = term if total is None else total + term
                    filtered[f, pl.ds(pl.multiple_of(r * fine + step * rows, rows), rows), cols] = total.astype(jnp.bfloat16)

    def write(f, slot):
        return pltpu.make_async_copy(stage.at[slot], out.at[:, f], out_sem.at[slot])

    @pl.loop(0, produced)
    def _(f):
        slot = lax.rem(f, 2)

        @pl.when(f >= 2)
        def _():
            write(f - 2, slot).wait()

        product = jnp.dot(table[...], filtered[f], preferred_element_type=jnp.float32)
        stage[slot] = product.astype(jnp.bfloat16).reshape(stage.shape[1:])
        write(f, slot).start()

    for f in (produced - 2, produced - 1):
        write(f, f % 2).wait()


def correlate(chips, span, history, inverse, received, out, turned_in, spectra, wide):
    width = received.shape[-1]
    groups = received.shape[1]
    total_inputs = groups * width
    frames = chips * span

    @pl.when(pl.program_id(0) == 0)
    def _():
        @pl.loop(0, chips // 2)
        def _(pair):
            for group in range(groups):
                column = (group % 2) * 2 + group // 2
                for lane in range(width // 128):
                    cols = pl.ds(lane * 128, 128)
                    for sub in range(2):
                        chip = pair * 2 + sub
                        for i in range(span):
                            value = received[chip, group, i, :, cols].astype(jnp.float32)
                            back = 1
                            while i + back * span < span + history:
                                earlier = received[jnp.maximum(chip - back, 0), group, i + back * span, :, cols].astype(jnp.float32)
                                value = value + jnp.where(chip >= back, earlier, 0.0)
                                back += 1
                            wide[pl.ds((sub * span + i) * 8, 8), :] = value
                    for row in range(8):
                        picked = wide[pl.ds(row, 2 * span, stride=8), :].astype(jnp.bfloat16)
                        here = pl.ds(pl.multiple_of((row % 2) * frames + pair * (2 * span), 2 * span), 2 * span)
                        there = pl.ds(pl.multiple_of((1 - row % 2) * frames + pair * (2 * span), 2 * span), 2 * span)
                        at = pl.ds(column * width + lane * 128, 128)
                        spectra[row // 2, here, at] = picked
                        turned_in[row // 2, there, at] = -picked if row % 2 else picked

    chan = pl.program_id(0)
    upper = lax.broadcasted_iota(jnp.int32, (width, width), 0) <= lax.broadcasted_iota(jnp.int32, (width, width), 1)
    contract = (((0,), (0,)), ((), ()))
    for a in range(total_inputs // width):
        rows = pl.ds(a * width, width)
        left = spectra[chan, :, rows]
        real = lax.dot_general(left, spectra[chan, :, pl.ds(a * width, total_inputs - a * width)], contract, preferred_element_type=jnp.float32)
        imag = lax.dot_general(left, turned_in[chan, :, pl.ds(0, (a + 1) * width)], contract, preferred_element_type=jnp.float32)
        if a:
            out[0, rows, pl.ds(0, a * width)] = (imag[:, : a * width] * inverse).astype(jnp.bfloat16)
        middle = jnp.where(upper, real[:, :width], imag[:, a * width :])
        out[0, rows, pl.ds(a * width, width)] = (middle * inverse).astype(jnp.bfloat16)
        if (a + 1) * width < total_inputs:
            out[0, rows, pl.ds((a + 1) * width, total_inputs - (a + 1) * width)] = (real[:, width:] * inverse).astype(jnp.bfloat16)


def per_device(voltages, taps):
    history = taps.shape[0] - 1
    fine = taps.shape[1]
    frames = voltages.shape[1] // fine
    width = voltages.shape[2]
    n_time = lax.axis_size("tm")
    n_group = lax.axis_size("inp")
    devices = n_time * n_group
    chans = KEEP // devices
    half = width // 2
    span = 2 * frames
    produced = span + history
    chips = n_time // 2
    scaled = (taps.astype(jnp.float32) * (1.0 / 8192.0)).T
    table = dft_rows(fine, KEEP)
    vmem = pl.BlockSpec(memory_space=pltpu.VMEM)
    hbm = pl.BlockSpec(memory_space=pl.ANY)
    parts = pl.pallas_call(
        functools.partial(partial_spectra, frames, fine, history),
        out_shape=jax.ShapeDtypeStruct((devices, produced, 2 * chans, half), jnp.bfloat16),
        in_specs=[hbm, vmem, vmem],
        out_specs=hbm,
        scratch_shapes=[
            pltpu.VMEM((span, 2, fine, half), jnp.bfloat16),
            pltpu.VMEM((produced, 2 * fine, half), jnp.bfloat16),
            pltpu.VMEM((2, devices, 2 * chans, half), jnp.bfloat16),
            pltpu.VMEM((history + 1, 16, 128), jnp.float32),
            pltpu.SemaphoreType.DMA((2, frames)),
            pltpu.SemaphoreType.DMA((2, frames)),
            pltpu.SemaphoreType.DMA((2, frames)),
            pltpu.SemaphoreType.DMA((2,)),
        ],
        compiler_params=pltpu.CompilerParams(collective_id=0, has_side_effects=True, vmem_limit_bytes=56 * 2**20),
        name="partial_spectra",
    )(voltages, scaled, table)
    flat = parts.reshape(devices, produced * 2 * chans, half)
    moved = lax.all_to_all(flat, ("tm", "inp"), split_axis=0, concat_axis=0, tiled=True)
    received = moved.reshape(chips, 2 * n_group, produced, 2 * chans, half)
    total = width * n_group
    return pl.pallas_call(
        functools.partial(correlate, chips, span, history, 1.0 / (chips * span)),
        out_shape=jax.ShapeDtypeStruct((chans, total, total), jnp.bfloat16),
        grid=(chans,),
        in_specs=[pl.BlockSpec(memory_space=pltpu.VMEM)],
        out_specs=pl.BlockSpec((1, total, total), lambda c: (c, 0, 0)),
        scratch_shapes=[
            pltpu.VMEM((chans, 2 * chips * span, total), jnp.bfloat16),
            pltpu.VMEM((chans, 2 * chips * span, total), jnp.bfloat16),
            pltpu.VMEM((2 * span * 8, 128), jnp.float32),
        ],
        compiler_params=pltpu.CompilerParams(vmem_limit_bytes=56 * 2**20),
        name="correlate",
    )(received)


def solution(mesh):
    placed = (P(None, "tm", "inp"), P())
    return jax.shard_map(
        per_device,
        mesh=mesh,
        in_specs=placed,
        out_specs=P(("tm", "inp"), None, None),
        check_vma=False,
    )
```

time: 762 us -> 212 us (0.28)
  waiting for transfers between devices: 431 us -> 0 us
  local copies, waits for them, and re-layouts: 149 us -> 5.14 us
  blocking collectives: 0 us -> 127 us
  starting transfers between devices: 94 us -> 0 us
  Pallas kernels: 0 us -> 72.1 us
  matrix products: 59.3 us -> 0 us
  other arithmetic: 24.9 us -> 7.09 us
    ppermute x3 -> x0, waiting for transfers between devices: 378 us -> none  [passed_along(): lax.ppermute(value, axis, [(source, source + steps) for source in range(f...]
    all_to_all x0 -> x1, blocking collectives: none -> 127 us  [per_device(): lax.all_to_all(flat, ('tm', 'inp'), split_axis=0, concat_axis=0, tiled=True)]
    all_to_all x1 -> x0, starting transfers between devices: 80 us -> none  [per_device(): lax.all_to_all(flat_spectra, ('tm', 'inp'), split_axis=0, concat_axis=2,...]
    pallas_call x0 -> x2, Pallas kernels: none -> 72.1 us  [the longest x1 56.4 us: per_device(): pl.pallas_call(functools.partial(partial_spectra, frames, fine, history),...]
    mul x2 -> x1, local copies, waits for them, and re-layouts: 68.8 us -> 1.01 us  [per_device(): scaled = (taps.astype(jnp.float32) * (1.0 / 8192.0)).T]
    dot_general x2 -> x0, matrix products: 59.3 us -> none  [the longest x1 38.9 us: per_device(): jnp.einsum('rfna,rnsj->jsfa', filtered, dft_matrix, preferred_element_typ...]
    all_to_all x1 -> x0, waiting for transfers between devices: 53.5 us -> none  [per_device(): lax.all_to_all(flat_spectra, ('tm', 'inp'), split_axis=0, concat_axis=2,...]
    reshape x3 -> x0, local copies, waits for them, and re-layouts: 30.2 us -> none  [the longest x1 11.4 us: per_device(): own_frames = voltages.reshape(2, frames, fine_count, input_width)]
  transfers between devices with their start and end apart: 4 -> 0, of which waited for: 2 -> 0; matrix products, arithmetic and copies ran while one was open for 4% -> 0% of each run, Pallas kernels for 0% -> 0%
where the time goes in v1:
time: 212 us; the launch traced here: 211 us
  blocking collectives  127 us (60%)
  Pallas kernels  72.1 us (34%)
  other arithmetic  7.09 us (3%)
  local copies, waits for them, and re-layouts  5.14 us (2%)
    all_to_all x1, blocking collectives, per_device(): lax.all_to_all(flat, ('tm', 'inp'), split_axis=0, concat_axis=0, tiled=True)  127 us
    pallas_call x1, Pallas kernels, per_device(): pl.pallas_call(functools.partial(partial_spectra, frames, fine, history),...  56.4 us
    pallas_call x1, Pallas kernels, per_device(): pl.pallas_call(functools.partial(correlate, chips, span, history, 1.0 / (...  15.7 us
    another operation x1, other arithmetic  5.56 us

profile of v1, /device:TPU:1, one launch (start us, length us, event | category | flops | bytes accessed | tf_op | source)
XLA Modules:
  0.0 211.4 jit_solution(15047536285022570006)
XLA Ops:
  0.0 0.8 convert_multiply_fusion
  0.8 1.0 copy.9
  1.9 5.6 %subtract_convert_fusion = (bf16[1024,1,8,128]{3,2,1,0:T(8,128)(2,1)S(1)}, bf16[1024,1,8,128]{3,2,1,0:T(8,128)(2,1)S(1)}) fusion(f32[1024,128]{1,0:T(8,128)} %constant.11.clone, f32[1024,8]{1,0:T(8,128)} %constant.13.clone, f32[1024,128]{1,0:T(8,128)} %constant.10.clone, f32[1024,8]{1,0:T(8,128)} %constant.12.clone), kind=kLoop, calls=%fused_computation.3 | loop fusion | flops 8388608 | bytes 5308416 | tf_op jit(solution)/shard_map/convert
  7.4 0.7 pad_maximum_fusion
  8.1 4.1 %copy.12 = bf16[128,8,16,128]{3,1,2,0:T(8,128)(2,1)} copy(bf16[128,8,16,128]{3,2,1,0:T(8,128)(2,1)S(1)} %bitcast.10) | data formatting | bytes 8388608
  12.2 56.4 %partial_spectra.1 = bf16[128,19,8,256]{3,2,1,0:T(8,128)(2,1)} custom-call(bf16[2,4096,512]{2,1,0:T(8,128)(2,1)} %volt.1, f32[1024,12]{1,0:T(8,128)} %bitcast.12, bf16[1024,2048]{1,0:T(8,128)(2,1)} %bitcast.11), custom_call_target="tpu_custom_call" | custom-call | tf_op jit(solution)/shard_map/partial_spectra/pallas_call | solution.py:180
  68.7 127.1 %all_to_all.5 = bf16[128,152,256]{2,1,0:T(8,128)(2,1)} all-to-all(bf16[128,152,256]{2,1,0:T(8,128)(2,1)} %bitcast.8), channel_id=1, replica_groups=mesh['tm'=64,'inp'=2] {'tm','inp'}, dimensions={0} | all-to-all | bytes 19922944 | tf_op jit(solution)/shard_map/all_to_all | solution.py:199
  195.8 15.7 %correlate.1 = bf16[4,1024,1024]{2,1,0:T(8,128)(2,1)} custom-call(bf16[32,4,19,8,256]{4,3,2,1,0:T(8,128)(2,1)} %bitcast.9), custom_call_target="tpu_custom_call" | custom-call | tf_op jit(solution)/shard_map/correlate/pallas_call | solution.py:202

commit v2 on v1

--- a/solution.py
+++ b/solution.py
@@ -26,52 +26,105 @@
     )
 
 
-def dft_rows(fine, keep):
-    low_cos, low_sin, high_cos, high_sin = (jnp.asarray(x) for x in table_parts(fine, keep))
-    first = high_cos[:, :, None] * low_cos[:, None, :] - high_sin[:, :, None] * low_sin[:, None, :]
-    second = high_sin[:, :, None] * low_cos[:, None, :] + high_cos[:, :, None] * low_sin[:, None, :]
-    rows = first.shape[0]
-    both = jnp.stack([first, second], axis=1)
-    return both.reshape(rows, 2 * fine).astype(jnp.bfloat16)
-
-
-def partial_spectra(frames, fine, history, volt, taps, table, out, samples, filtered, stage, wide_taps, in_sem, send_sem, recv_sem, out_sem):
-    me = lax.axis_index("tm")
-    core = lax.rem(me, 2)
-    other = 1 - core
-    partner = me + 1 - 2 * core
+CHUNKS = (2, 3, 3, 3, 3, 3, 2)
+STEP_BACK = 3
+
+
+class Place:
+    def __init__(self):
+        time, self.z_lo = lax.axis_index("tm"), lax.axis_index("inp")
+        self.core, self.y = lax.rem(time, 2), lax.rem(time // 2, 4)
+        self.x, self.z_hi = lax.rem(time // 8, 4), time // 32
+
+    def index(self, z_lo, core, y, x, z_hi):
+        return ((z_hi * 4 + x) * 4 + y) * 2 + core, z_lo
+
+    def mixed(self, own, digit):
+        low = lax.rem(own + digit, 2)
+        high = lax.rem(own // 2 + digit // 2, 2)
+        return high * 2 + low
+
+    def flipped(self, flip):
+        z_lo, core, y, x, z_hi = flip
+        return self.index(
+            lax.rem(self.z_lo + z_lo, 2), lax.rem(self.core + core, 2), self.mixed(self.y, y), self.mixed(self.x, x), lax.rem(self.z_hi + z_hi, 2)
+        )
+
+    def shifted(self, flip, shift, mix):
+        z_lo, core, y, x, z_hi = flip
+        moved_y = lax.rem(self.y + shift, 4)
+        moved_x = lax.rem(self.x + shift, 4)
+        moved_z = lax.rem(self.z_hi * 2 + self.z_lo + shift, 4)
+        new_y = moved_y if y == 2 else (self.mixed(self.y, y) if mix else self.y)
+        other_x = self.mixed(self.x, x) if mix else self.x
+        new_x = jnp.where(x == 2, moved_x, other_x)
+        other_lo = lax.rem(self.z_lo + z_lo, 2) if mix else self.z_lo
+        other_hi = lax.rem(self.z_hi + z_hi, 2) if mix else self.z_hi
+        if z_lo:
+            new_lo, new_hi = other_lo, other_hi
+        else:
+            new_lo = jnp.where(z_hi == 1, lax.rem(moved_z, 2), other_lo)
+            new_hi = jnp.where(z_hi == 1, moved_z // 2, other_hi)
+        new_core = lax.rem(self.core + core, 2) if mix else self.core
+        return self.index(new_lo, new_core, new_y, new_x, new_hi)
+
+
+def far(flip):
+    z_lo, _, y, x, z_hi = flip
+    if y == 2:
+        return True
+    return (x == 2) if z_lo else jnp.logical_or(x == 2, z_hi == 1)
+
+
+def both(first, second):
+    return {"tm": first, "inp": second}
+
+
+def when(condition, action):
+    if condition is True:
+        action()
+    else:
+        pl.when(condition)(action)
+
+
+def each_flip(action):
+    @pl.loop(0, 8)
+    def _(outer):
+        x, z_hi = lax.rem(outer, 4), outer // 4
+        for inner in range(16):
+            flip = (inner % 2, (inner // 2) % 2, inner // 4, x, z_hi)
+            if inner == 0:
+                pl.when(outer > 0)(functools.partial(action, flip))
+            else:
+                action(flip)
+
+
+def spread_spectra(
+    frames, fine, history, volt, taps, low_cos, low_sin, high_cos, high_sin, out,
+    samples, filtered, stage, relay, table, wide_taps, in_sem, give_sem, send_sem, relay_sem, pass_sem, recv_sem, own_sem,
+):
+    place = Place()
+    me = lax.axis_index("tm") * 2 + lax.axis_index("inp")
+    core = place.core
+    partner = lax.axis_index("tm") + 1 - 2 * core
     span = 2 * frames
     produced = span + history
     half = samples.shape[3]
+    devices = stage.shape[0]
     barrier = pltpu.get_barrier_semaphore()
-    pl.semaphore_signal(barrier, inc=1, device_id={"tm": partner}, device_id_type=MESH)
-    pl.semaphore_wait(barrier, 1)
+
+    def greet(flip):
+        pl.semaphore_signal(barrier, inc=1, device_id=both(*place.flipped(flip)), device_id_type=MESH)
+
+    each_flip(greet)
 
     def lanes(which):
         return pl.ds(pl.multiple_of(which * half, half), half)
 
-    remote = []
-    local = []
-    for r in range(2):
-        for f in range(frames):
-            source = volt.at[r, pl.ds(f * fine, fine)]
-            remote.append(
-                pltpu.make_async_remote_copy(
-                    src_ref=source.at[:, lanes(other)],
-                    dst_ref=samples.at[core * frames + f, r],
-                    send_sem=send_sem.at[r, f],
-                    recv_sem=recv_sem.at[r, f],
-                    device_id={"tm": partner},
-                    device_id_type=MESH,
-                )
-            )
-            local.append(
-                pltpu.make_async_copy(source.at[:, lanes(core)], samples.at[core * frames + f, r], in_sem.at[r, f])
-            )
-    for copy in remote + local:
-        copy.start()
-    for copy in local + remote:
-        copy.wait()
+    order = [(f, r) for f in range(frames) for r in range(2)]
+    for f, r in order:
+        source = volt.at[r, pl.ds(f * fine, fine), lanes(core)]
+        pltpu.make_async_copy(source, samples.at[core * frames + f, r], in_sem.at[core * frames + f, r]).start()
 
     rows = 16
 
@@ -80,36 +133,141 @@
         at = pl.ds(pl.multiple_of(step * rows, rows), rows)
         tap_rows = taps[at, :]
         for k in range(history + 1):
-            wide_taps[k] = jnp.broadcast_to(tap_rows[:, k : k + 1], (rows, 128))
-        for r in range(2):
-            for lane in range(half // 128):
-                cols = pl.ds(lane * 128, 128)
-                held = [samples[i, r, at, cols].astype(jnp.float32) for i in range(span)]
-                for f in range(produced):
-                    total = None
-                    for i in range(span):
-                        if 0 <= f - i <= history:
-                            term = wide_taps[f - i] * held[i]
-                            total = term if total is None else total + term
-                    filtered[f, pl.ds(pl.multiple_of(r * fine + step * rows, rows), rows), cols] = total.astype(jnp.bfloat16)
-
-    def write(f, slot):
-        return pltpu.make_async_copy(stage.at[slot], out.at[:, f], out_sem.at[slot])
-
-    @pl.loop(0, produced)
-    def _(f):
-        slot = lax.rem(f, 2)
-
-        @pl.when(f >= 2)
-        def _():
-            write(f - 2, slot).wait()
-
-        product = jnp.dot(table[...], filtered[f], preferred_element_type=jnp.float32)
-        stage[slot] = product.astype(jnp.bfloat16).reshape(stage.shape[1:])
-        write(f, slot).start()
-
-    for f in (produced - 2, produced - 1):
-        write(f, f % 2).wait()
+            wide_taps[k, at] = jnp.broadcast_to(tap_rows[:, k : k + 1], (rows, 128))
+
+    @pl.loop(0, table.shape[0] // rows)
+    def _(step):
+        at = pl.ds(pl.multiple_of(step * rows, rows), rows)
+        base_cos, base_sin = low_cos[at, :], low_sin[at, :]
+        more_cos, more_sin = high_cos[at, :], high_sin[at, :]
+        for block in range(fine // 128):
+            turn_cos = jnp.broadcast_to(more_cos[:, block : block + 1], (rows, 128))
+            turn_sin = jnp.broadcast_to(more_sin[:, block : block + 1], (rows, 128))
+            table[at, pl.ds(block * 128, 128)] = (turn_cos * base_cos - turn_sin * base_sin).astype(jnp.bfloat16)
+            table[at, pl.ds(fine + block * 128, 128)] = (turn_sin * base_cos + turn_cos * base_sin).astype(jnp.bfloat16)
+
+    pl.semaphore_wait(barrier, devices - 1)
+
+    given = []
+    for f, r in order:
+        given.append(
+            pltpu.make_async_remote_copy(
+                src_ref=volt.at[r, pl.ds(f * fine, fine), lanes(1 - core)],
+                dst_ref=samples.at[core * frames + f, r],
+                send_sem=give_sem.at[f, r],
+                recv_sem=in_sem.at[core * frames + f, r],
+                device_id={"tm": partner},
+                device_id_type=MESH,
+            )
+        )
+        given[-1].start()
+
+    def send(chunk, piece, flip):
+        first, second = place.flipped(flip)
+
+        def straight():
+            pltpu.make_async_remote_copy(
+                src_ref=stage.at[first * 2 + second, piece],
+                dst_ref=out.at[me, piece],
+                send_sem=send_sem,
+                recv_sem=recv_sem,
+                device_id=both(first, second),
+                device_id_type=MESH,
+            ).start()
+
+        def relayed():
+            z_lo, _, y, x, z_hi = flip
+            pltpu.make_async_remote_copy(
+                src_ref=stage.at[first * 2 + second, piece],
+                dst_ref=relay.at[((z_hi * 4 + x) * 4 + y) * 2 + z_lo, piece],
+                send_sem=send_sem,
+                recv_sem=relay_sem.at[chunk],
+                device_id=both(*place.shifted(flip, STEP_BACK, False)),
+                device_id_type=MESH,
+            ).start()
+
+        if flip[1] == 0:
+            straight()
+        else:
+            is_far = far(flip)
+            when(is_far, relayed)
+            if is_far is not True:
+                pl.when(jnp.logical_not(is_far))(straight)
+
+    def pass_on(chunk, piece):
+        waited = relay.at[pl.ds(0, 37), piece]
+        pltpu.make_async_copy(waited, waited, relay_sem.at[chunk]).wait()
+
+        def forward(flip):
+            if flip[1] == 0:
+                return
+            z_lo, _, y, x, z_hi = flip
+            came_time, came_lo = place.shifted(flip, 4 - STEP_BACK, False)
+
+            def go():
+                pltpu.make_async_remote_copy(
+                    src_ref=relay.at[((z_hi * 4 + x) * 4 + y) * 2 + z_lo, piece],
+                    dst_ref=out.at[came_time * 2 + came_lo, piece],
+                    send_sem=pass_sem,
+                    recv_sem=recv_sem,
+                    device_id=both(*place.shifted(flip, STEP_BACK, True)),
+                    device_id_type=MESH,
+                ).start()
+
+            when(far(flip), go)
+
+        each_flip(forward)
+
+    begin = 0
+    pieces = []
+    arrived = 0
+    for chunk, count in enumerate(CHUNKS):
+        end = begin + count
+        while arrived < min(span, end):
+            for r in range(2):
+                pltpu.make_async_copy(samples.at[arrived, r], samples.at[arrived, r], in_sem.at[arrived, r]).wait()
+            arrived += 1
+        inputs = [i for i in range(span) if begin - history <= i < end]
+
+        @pl.loop(0, fine // rows)
+        def _(step):
+            at = pl.ds(pl.multiple_of(step * rows, rows), rows)
+            for r in range(2):
+                for lane in range(half // 128):
+                    cols = pl.ds(lane * 128, 128)
+                    held = {i: samples[i, r, at, cols].astype(jnp.float32) for i in inputs}
+                    for f in range(begin, end):
+                        total = None
+                        for i in inputs:
+                            if 0 <= f - i <= history:
+                                term = wide_taps[f - i, at] * held[i]
+                                total = term if total is None else total + term
+                        filtered[f - begin, pl.ds(pl.multiple_of(r * fine + step * rows, rows), rows), cols] = total.astype(jnp.bfloat16)
+
+        @pl.loop(0, count)
+        def _(f):
+            product = jnp.dot(table[...], filtered[f], preferred_element_type=jnp.float32)
+            stage[:, begin + f] = product.astype(jnp.bfloat16).reshape(devices, stage.shape[2], half)
+
+        piece = pl.ds(begin, count)
+        pieces.append(piece)
+        each_flip(functools.partial(send, chunk, piece))
+        if chunk >= 1:
+            pass_on(chunk - 1, pieces[chunk - 1])
+        begin = end
+
+    own = pltpu.make_async_copy(stage.at[me], out.at[me], own_sem)
+    own.start()
+    pass_on(len(CHUNKS) - 1, pieces[-1])
+    own.wait()
+    for copy in given:
+        copy.wait_send()
+    sent = stage.at[pl.ds(0, devices - 1)]
+    pltpu.make_async_copy(sent, sent, send_sem).wait()
+    passed = relay.at[pl.ds(0, 37)]
+    pltpu.make_async_copy(passed, passed, pass_sem).wait()
+    taken = out.at[pl.ds(0, devices - 1)]
+    pltpu.make_async_copy(taken, taken, recv_sem).wait()
 
 
 def correlate(chips, span, history, inverse, received, out, turned_in, spectra, wide):
@@ -174,29 +332,32 @@
     produced = span + history
     chips = n_time // 2
     scaled = (taps.astype(jnp.float32) * (1.0 / 8192.0)).T
-    table = dft_rows(fine, KEEP)
+    tables = [jnp.asarray(x) for x in table_parts(fine, KEEP)]
     vmem = pl.BlockSpec(memory_space=pltpu.VMEM)
     hbm = pl.BlockSpec(memory_space=pl.ANY)
-    parts = pl.pallas_call(
-        functools.partial(partial_spectra, frames, fine, history),
+    moved = pl.pallas_call(
+        functools.partial(spread_spectra, frames, fine, history),
         out_shape=jax.ShapeDtypeStruct((devices, produced, 2 * chans, half), jnp.bfloat16),
-        in_specs=[hbm, vmem, vmem],
+        in_specs=[hbm] + [vmem] * 5,
         out_specs=hbm,
         scratch_shapes=[
             pltpu.VMEM((span, 2, fine, half), jnp.bfloat16),
-            pltpu.VMEM((produced, 2 * fine, half), jnp.bfloat16),
-            pltpu.VMEM((2, devices, 2 * chans, half), jnp.bfloat16),
-            pltpu.VMEM((history + 1, 16, 128), jnp.float32),
-            pltpu.SemaphoreType.DMA((2, frames)),
-            pltpu.SemaphoreType.DMA((2, frames)),
-            pltpu.SemaphoreType.DMA((2, frames)),
-            pltpu.SemaphoreType.DMA((2,)),
+            pltpu.VMEM((max(CHUNKS), 2 * fine, half), jnp.bfloat16),
+            pltpu.VMEM((devices, produced, 2 * chans, half), jnp.bfloat16),
+            pltpu.VMEM((devices // 2, produced, 2 * chans, half), jnp.bfloat16),
+            pltpu.VMEM((2 * KEEP, 2 * fine), jnp.bfloat16),
+            pltpu.VMEM((history + 1, fine, 128), jnp.float32),
+            pltpu.SemaphoreType.DMA((span, 2)),
+            pltpu.SemaphoreType.DMA((frames, 2)),
+            pltpu.SemaphoreType.DMA,
+            pltpu.SemaphoreType.DMA((len(CHUNKS),)),
+            pltpu.SemaphoreType.DMA,
+            pltpu.SemaphoreType.DMA,
+            pltpu.SemaphoreType.DMA,
         ],
-        compiler_params=pltpu.CompilerParams(collective_id=0, has_side_effects=True, vmem_limit_bytes=56 * 2**20),
-        name="partial_spectra",
-    )(voltages, scaled, table)
-    flat = parts.reshape(devices, produced * 2 * chans, half)
-    moved = lax.all_to_all(flat, ("tm", "inp"), split_axis=0, concat_axis=0, tiled=True)
+        compiler_params=pltpu.CompilerParams(collective_id=0, has_side_effects=True, vmem_limit_bytes=58 * 2**20),
+        name="spread_spectra",
+    )(voltages, scaled, *tables)
     received = moved.reshape(chips, 2 * n_group, produced, 2 * chans, half)
     total = width * n_group
     return pl.pallas_call(

time: 212 us -> 186 us (0.88)
  blocking collectives: 127 us -> 0 us
  Pallas kernels: 72.1 us -> 183 us
  other arithmetic: 7.09 us -> 0.85 us
  local copies, waits for them, and re-layouts: 5.14 us -> 1.02 us
    all_to_all x1 -> x0, blocking collectives: 127 us -> none  [per_device(): lax.all_to_all(flat, ('tm', 'inp'), split_axis=0, concat_axis=0, tiled=True)]
    pallas_call x1, Pallas kernels: 56.4 us -> 168 us  [per_device(): pl.pallas_call(functools.partial(spread_spectra, frames, fine, history),...]
    another operation x2 -> x0, other arithmetic: 6.24 us -> none
    unnamed x1 -> x0, local copies, waits for them, and re-layouts: 4.13 us -> none
where the time goes in v2:
time: 186 us; the launch traced here: 185 us
  Pallas kernels  183 us (98%)
    pallas_call x1, Pallas kernels, per_device(): pl.pallas_call(functools.partial(spread_spectra, frames, fine, history),...  168 us
    pallas_call x1, Pallas kernels, per_device(): pl.pallas_call(functools.partial(correlate, chips, span, history, 1.0 / (...  15.7 us

profile of v2, /device:TPU:1, one launch (start us, length us, event | category | flops | bytes accessed | tf_op | source)
XLA Modules:
  0.0 185.2 jit_solution(10072974692500209279)
XLA Ops:
  0.0 0.8 convert_multiply_fusion
  0.8 1.0 copy.9
  1.9 167.6 %spread_spectra.1 = bf16[128,19,8,256]{3,2,1,0:T(8,128)(2,1)} custom-call(bf16[2,4096,512]{2,1,0:T(8,128)(2,1)} %volt.1, f32[1024,12]{1,0:T(8,128)} %bitcast.3, f32[1024,128]{1,0:T(8,128)} %constant.10.clone.low_cos, f32[1024,128]{1,0:T(8,128)} %constant.11.clone.low_sin, f32[1024,8]{1,0:T(8,128)} %constant.12.clone.high_cos, f32[1024,8]{1,0:T(8,128)} %constant.13.clone.high_sin), custom_call_target="tpu_custom_call" | custom-call | tf_op jit(solution)/shard_map/spread_spectra/pallas_call | solution.py:338
  169.5 15.7 %correlate.1 = bf16[4,1024,1024]{2,1,0:T(8,128)(2,1)} custom-call(bf16[32,4,19,8,256]{4,3,2,1,0:T(8,128)(2,1)} %bitcast.2), custom_call_target="tpu_custom_call" | custom-call | tf_op jit(solution)/shard_map/correlate/pallas_call | solution.py:363

commit v3 on v2

v3 whole, which is shorter than its diff:
```python
import functools
import math

import jax
import jax.numpy as jnp
import numpy as np
from jax import lax
from jax.experimental import pallas as pl
from jax.experimental.pallas import tpu as pltpu
from jax.sharding import PartitionSpec as P

KEEP = 512
MESH = pl.DeviceIdType.MESH


UNITS = ((0, 1, 2), (8, 16), (9, 17), (10, 18), (3, 11), (4, 12), (5, 13), (6, 14), (7, 15))
RING = 4


def table_parts(fine, keep, owned):
    chan = (np.arange(keep) - keep // 2).reshape(-1, RING, 4 * owned)
    chan = np.repeat(chan.transpose(1, 0, 2).reshape(-1), 2)
    part = np.tile(np.arange(2), keep)
    low = (chan[:, None] * np.arange(128)[None, :] + part[:, None] * (fine // 4)) % fine
    high = (chan[:, None] * np.arange(0, fine, 128)[None, :]) % fine
    scale = 1.0 / math.sqrt(fine)
    step = 2.0 * np.pi / fine
    return tuple(
        x.astype(np.float32)
        for x in (np.cos(step * low) * scale, np.sin(step * low) * scale, np.cos(step * high), np.sin(step * high))
    )


def row_slots(span, history):
    slots, count = {}, 0
    for q in range(span):
        for m in range(RING + (history + span - 1 - q) // span):
            slots[q, m] = count
            count += 1
    return slots, count


class Place:
    def __init__(self):
        time, self.z_lo = lax.axis_index("tm"), lax.axis_index("inp")
        self.core, self.y = lax.rem(time, 2), lax.rem(time // 2, RING)
        self.x, self.z_hi = lax.rem(time // 8, 4), time // 32

    def device(self, y, x, z_hi, core, z_lo):
        return {"tm": ((z_hi * 4 + x) * RING + y) * 2 + core, "inp": z_lo}

    def along(self, steps):
        return self.device(lax.rem(self.y + steps + RING, RING), self.x, self.z_hi, self.core, self.z_lo)

    def flipped(self, flip):
        x_flip, z_hi_flip, core_flip, z_lo_flip = flip
        x = lax.rem(self.x // 2 + x_flip // 2, 2) * 2 + lax.rem(self.x + x_flip, 2)
        z_hi = lax.rem(self.z_hi + z_hi_flip, 2)
        core, z_lo = lax.rem(self.core + core_flip, 2), lax.rem(self.z_lo + z_lo_flip, 2)
        return self.device(self.y, x, z_hi, core, z_lo), ((z_hi * 4 + x) * 2 + core) * 2 + z_lo

    def number(self):
        return ((self.z_hi * 4 + self.x) * 2 + self.core) * 2 + self.z_lo


def each_flip(action):
    @pl.loop(0, 8)
    def _(outer):
        for inner in range(4):
            flip = (lax.rem(outer, 4), outer // 4, inner % 2, inner // 2)
            if inner == 0:
                pl.when(outer > 0)(functools.partial(action, flip))
            else:
                action(flip)


def spread_spectra(
    frames, fine, history, volt, taps, low_cos, low_sin, high_cos, high_sin, out,
    samples, filtered, stage, heard, relay, summed, table, wide_taps,
    in_sem, give_sem, send_sem, relay_sem, pass_sem, heard_sem, keep_sem, plane_sem, recv_sem, own_sem,
):
    place = Place()
    core, here = place.core, place.number()
    partner = lax.axis_index("tm") + 1 - 2 * core
    span = 2 * frames
    half = samples.shape[3]
    plane = summed.shape[0]
    slots, _ = row_slots(span, history)
    order = [f for unit in UNITS for f in unit]
    slot_of = {f: i for i, f in enumerate(order)}
    barrier = pltpu.get_barrier_semaphore()

    def greet(flip):
        pl.semaphore_signal(barrier, inc=1, device_id=place.flipped(flip)[0], device_id_type=MESH)

    each_flip(greet)
    for steps in (1, -1):
        pl.semaphore_signal(barrier, inc=1, device_id=place.along(steps), device_id_type=MESH)

    def lanes(which):
        return pl.ds(pl.multiple_of(which * half, half), half)

    pieces = [(f, r) for f in range(frames) for r in range(2)]
    for f, r in pieces:
        source = volt.at[r, pl.ds(f * fine, fine), lanes(core)]
        pltpu.make_async_copy(source, samples.at[core * frames + f, r], in_sem.at[core * frames + f, r]).start()

    rows = 16

    @pl.loop(0, fine // rows)
    def _(step):
        at = pl.ds(pl.multiple_of(step * rows, rows), rows)
        tap_rows = taps[at, :]
        for k in range(history + 1):
            wide_taps[k, at] = jnp.broadcast_to(tap_rows[:, k : k + 1], (rows, 128))

    pl.semaphore_wait(barrier, plane + 1)

    given = []
    for f, r in pieces:
        given.append(
            pltpu.make_async_remote_copy(
                src_ref=volt.at[r, pl.ds(f * fine, fine), lanes(1 - core)],
                dst_ref=samples.at[core * frames + f, r],
                send_sem=give_sem.at[f, r],
                recv_sem=in_sem.at[core * frames + f, r],
                device_id={"tm": partner},
                device_id_type=MESH,
            )
        )
        given[-1].start()

    @pl.loop(0, table.shape[0] // rows)
    def _(step):
        at = pl.ds(pl.multiple_of(step * rows, rows), rows)
        base_cos, base_sin = low_cos[at, :], low_sin[at, :]
        more_cos, more_sin = high_cos[at, :], high_sin[at, :]
        for block in range(fine // 128):
            turn_cos = jnp.broadcast_to(more_cos[:, block : block + 1], (rows, 128))
            turn_sin = jnp.broadcast_to(more_sin[:, block : block + 1], (rows, 128))
            table[at, pl.ds(block * 128, 128)] = (turn_cos * base_cos - turn_sin * base_sin).astype(jnp.bfloat16)
            table[at, pl.ds(fine + block * 128, 128)] = (turn_sin * base_cos + turn_cos * base_sin).astype(jnp.bfloat16)

    def remote(source, target, send, recv, device):
        pltpu.make_async_remote_copy(
            src_ref=source, dst_ref=target, send_sem=send, recv_sem=recv, device_id=device, device_id_type=MESH
        ).start()

    hops = ((0, 1), (1, -1))

    def half_of(side):
        return pl.ds(side * (plane // 2), plane // 2)

    def send(unit, at):
        across = lax.rem(place.y + 2, RING)
        for side, steps in hops:
            remote(stage.at[at, across, half_of(side)], relay.at[at, side], send_sem, relay_sem.at[unit], place.along(steps))
        for side, steps in hops:
            to = lax.rem(place.y + steps + RING, RING)
            remote(stage.at[at, to], heard.at[at, place.y], send_sem, heard_sem.at[unit], place.along(steps))
        pltpu.make_async_copy(stage.at[at, place.y], heard.at[at, place.y], keep_sem.at[unit]).start()

    def pass_on(unit, at):
        pltpu.make_async_copy(relay.at[at], relay.at[at], relay_sem.at[unit]).wait()
        for side, steps in hops:
            came = lax.rem(place.y - steps + RING, RING)
            remote(relay.at[at, side], heard.at[at, came, half_of(side)], pass_sem, heard_sem.at[unit], place.along(steps))

    def hear(unit, at):
        three = heard.at[at, pl.ds(0, RING - 1)]
        pltpu.make_async_copy(three, three, heard_sem.at[unit]).wait()
        one = heard.at[at, 0]
        pltpu.make_async_copy(one, one, keep_sem.at[unit]).wait()

    def finish(q):
        ms = [m for (other, m) in slots if other == q]
        locals_ = [f for f in range(q, span + history, span)]

        @pl.loop(0, plane)
        def _(device):
            for m in ms:
                total = None
                for j, f in enumerate(locals_):
                    if 0 <= m - j < RING:
                        term = heard[slot_of[f], m - j, device].astype(jnp.float32)
                        total = term if total is None else total + term
                summed[device, slots[q, m]] = total.astype(jnp.bfloat16)

        piece = pl.ds(slots[q, 0], len(ms))

        def spread(flip):
            device, number = place.flipped(flip)
            remote(summed.at[number, piece], out.at[here, piece], plane_sem, recv_sem, device)

        each_flip(spread)

    at = []
    begin = 0
    arrived = 0
    for unit, outputs in enumerate(UNITS):
        count = len(outputs)
        while arrived <= min(span - 1, max(outputs)):
            for r in range(2):
                pltpu.make_async_copy(samples.at[arrived, r], samples.at[arrived, r], in_sem.at[arrived, r]).wait()
            arrived += 1
        inputs = [i for i in range(span) if any(0 <= f - i <= history for f in outputs)]

        @pl.loop(0, fine // rows)
        def _(step):
            here_rows = pl.ds(pl.multiple_of(step * rows, rows), rows)
            for r in range(2):
                for lane in range(half // 128):
                    cols = pl.ds(lane * 128, 128)
                    held = {i: samples[i, r, here_rows, cols].astype(jnp.float32) for i in inputs}
                    for place_in, f in enumerate(outputs):
                        total = None
                        for i in inputs:
                            if 0 <= f - i <= history:
                                term = wide_taps[f - i, here_rows] * held[i]
                                total = term if total is None else total + term
                        filtered[place_in, pl.ds(pl.multiple_of(r * fine + step * rows, rows), rows), cols] = total.astype(jnp.bfloat16)

        @pl.loop(0, count)
        def _(f):
            product = jnp.dot(table[...], filtered[f], preferred_element_type=jnp.float32)
            stage[begin + f] = product.astype(jnp.bfloat16).reshape(stage.shape[1:])

        at.append(pl.ds(begin, count))
        send(unit, at[unit])
        if unit >= 1:
            pass_on(unit - 1, at[unit - 1])
        if unit >= 2:
            hear(unit - 2, at[unit - 2])
        if unit >= 3:
            finish(UNITS[unit - 2][0] % span)
        begin += count

    last = len(UNITS) - 1
    pass_on(last, at[last])
    for unit in (last - 1, last):
        hear(unit, at[unit])
        finish(UNITS[unit][0] % span)
    own = pltpu.make_async_copy(summed.at[here], out.at[here], own_sem)
    own.start()
    own.wait()
    for copy in given:
        copy.wait_send()
    sent = stage.at[:, pl.ds(0, RING - 1)]
    pltpu.make_async_copy(sent, sent, send_sem).wait()
    pltpu.make_async_copy(relay, relay, pass_sem).wait()
    others = summed.at[pl.ds(0, plane - 1)]
    pltpu.make_async_copy(others, others, plane_sem).wait()
    taken = out.at[pl.ds(0, plane - 1)]
    pltpu.make_async_copy(taken, taken, recv_sem).wait()


def correlate(span, history, inverse, received, out, turned_in, spectra, wide):
    lines, groups = received.shape[:2]
    width = received.shape[-1]
    total_inputs = groups * width
    frames = lines * RING * span
    slots, _ = row_slots(span, history)

    @pl.when(pl.program_id(0) == 0)
    def _():
        @pl.loop(0, lines)
        def _(line):
            for pair in range(RING // 2):
                for group in range(groups):
                    column = (group % 2) * 2 + group // 2
                    for lane in range(width // 128):
                        cols = pl.ds(lane * 128, 128)
                        for sub in range(2):
                            m = pair * 2 + sub
                            for q in range(span):
                                value = received[line, group, slots[q, m], :, cols].astype(jnp.float32)
                                if (q, m + RING) in slots:
                                    earlier = received[jnp.maximum(line - 1, 0), group, slots[q, m + RING], :, cols]
                                    value = value + jnp.where(line > 0, earlier.astype(jnp.float32), 0.0)
                                wide[pl.ds((sub * span + q) * 8, 8), :] = value
                        for row in range(8):
                            picked = wide[pl.ds(row, 2 * span, stride=8), :].astype(jnp.bfloat16)
                            first = line * (RING * span) + pair * 2 * span
                            here = pl.ds(pl.multiple_of((row % 2) * frames + first, 2 * span), 2 * span)
                            there = pl.ds(pl.multiple_of((1 - row % 2) * frames + first, 2 * span), 2 * span)
                            at = pl.ds(column * width + lane * 128, 128)
                            spectra[row // 2, here, at] = picked
                            turned_in[row // 2, there, at] = -picked if row % 2 else picked

    chan = pl.program_id(0)
    upper = lax.broadcasted_iota(jnp.int32, (width, width), 0) <= lax.broadcasted_iota(jnp.int32, (width, width), 1)
    contract = (((0,), (0,)), ((), ()))
    for a in range(total_inputs // width):
        rows = pl.ds(a * width, width)
        left = spectra[chan, :, rows]
        real = lax.dot_general(left, spectra[chan, :, pl.ds(a * width, total_inputs - a * width)], contract, preferred_element_type=jnp.float32)
        imag = lax.dot_general(left, turned_in[chan, :, pl.ds(0, (a + 1) * width)], contract, preferred_element_type=jnp.float32)
        if a:
            out[0, rows, pl.ds(0, a * width)] = (imag[:, : a * width] * inverse).astype(jnp.bfloat16)
        middle = jnp.where(upper, real[:, :width], imag[:, a * width :])
        out[0, rows, pl.ds(a * width, width)] = (middle * inverse).astype(jnp.bfloat16)
        if (a + 1) * width < total_inputs:
            out[0, rows, pl.ds((a + 1) * width, total_inputs - (a + 1) * width)] = (real[:, width:] * inverse).astype(jnp.bfloat16)


def per_device(voltages, taps):
    history = taps.shape[0] - 1
    fine = taps.shape[1]
    frames = voltages.shape[1] // fine
    width = voltages.shape[2]
    n_time = lax.axis_size("tm")
    n_group = lax.axis_size("inp")
    devices = n_time * n_group
    chans = KEEP // devices
    half = width // 2
    span = 2 * frames
    produced = span + history
    plane = devices // RING
    lines = plane // 4
    rows_kept = row_slots(span, history)[1]
    scaled = (taps.astype(jnp.float32) * (1.0 / 8192.0)).T
    tables = [jnp.asarray(x) for x in table_parts(fine, KEEP, chans)]
    vmem = pl.BlockSpec(memory_space=pltpu.VMEM)
    hbm = pl.BlockSpec(memory_space=pl.ANY)
    block = (2 * chans, half)
    biggest = max(len(unit) for unit in UNITS)
    moved = pl.pallas_call(
        functools.partial(spread_spectra, frames, fine, history),
        out_shape=jax.ShapeDtypeStruct((plane, rows_kept, *block), jnp.bfloat16),
        in_specs=[hbm] + [vmem] * 5,
        out_specs=hbm,
        scratch_shapes=[
            pltpu.VMEM((span, 2, fine, half), jnp.bfloat16),
            pltpu.VMEM((biggest, 2 * fine, half), jnp.bfloat16),
            pltpu.VMEM((produced, RING, plane, *block), jnp.bfloat16),
            pltpu.VMEM((produced, RING, plane, *block), jnp.bfloat16),
            pltpu.VMEM((produced, 2, plane // 2, *block), jnp.bfloat16),
            pltpu.VMEM((plane, rows_kept, *block), jnp.bfloat16),
            pltpu.VMEM((2 * KEEP, 2 * fine), jnp.bfloat16),
            pltpu.VMEM((history + 1, fine, 128), jnp.float32),
            pltpu.SemaphoreType.DMA((span, 2)),
            pltpu.SemaphoreType.DMA((frames, 2)),
            pltpu.SemaphoreType.DMA,
            pltpu.SemaphoreType.DMA((len(UNITS),)),
            pltpu.SemaphoreType.DMA,
            pltpu.SemaphoreType.DMA((len(UNITS),)),
            pltpu.SemaphoreType.DMA((len(UNITS),)),
            pltpu.SemaphoreType.DMA,
            pltpu.SemaphoreType.DMA,
            pltpu.SemaphoreType.DMA,
        ],
        compiler_params=pltpu.CompilerParams(collective_id=0, has_side_effects=True, vmem_limit_bytes=60 * 2**20),
        name="spread_spectra",
    )(voltages, scaled, *tables)
    received = moved.reshape(lines, 2 * n_group, rows_kept, *block)
    total = width * n_group
    return pl.pallas_call(
        functools.partial(correlate, span, history, 1.0 / (n_time * frames)),
        out_shape=jax.ShapeDtypeStruct((chans, total, total), jnp.bfloat16),
        grid=(chans,),
        in_specs=[pl.BlockSpec(memory_space=pltpu.VMEM)],
        out_specs=pl.BlockSpec((1, total, total), lambda c: (c, 0, 0)),
        scratch_shapes=[
            pltpu.VMEM((chans, 2 * n_time * frames, total), jnp.bfloat16),
            pltpu.VMEM((chans, 2 * n_time * frames, total), jnp.bfloat16),
            pltpu.VMEM((2 * span * 8, 128), jnp.float32),
        ],
        compiler_params=pltpu.CompilerParams(vmem_limit_bytes=56 * 2**20),
        name="correlate",
    )(received)


def solution(mesh):
    placed = (P(None, "tm", "inp"), P())
    return jax.shard_map(
        per_device,
        mesh=mesh,
        in_specs=placed,
        out_specs=P(("tm", "inp"), None, None),
        check_vma=False,
    )
```

time: 186 us -> 167 us (0.90)
  Pallas kernels: 183 us -> 165 us
    pallas_call x1, Pallas kernels: 168 us -> 151 us  [per_device(): pl.pallas_call(functools.partial(spread_spectra, frames, fine, history),...]
    pallas_call x1, Pallas kernels: 15.7 us -> 13.6 us  [per_device(): pl.pallas_call(functools.partial(correlate, span, history, 1.0 / (n_time...]
where the time goes in v3:
time: 167 us
  Pallas kernels  165 us (99%)
    pallas_call x1, Pallas kernels, per_device(): pl.pallas_call(functools.partial(spread_spectra, frames, fine, history),...  151 us
    pallas_call x1, Pallas kernels, per_device(): pl.pallas_call(functools.partial(correlate, span, history, 1.0 / (n_time...  13.6 us

profile of v3, /device:TPU:1, one launch (start us, length us, event | category | flops | bytes accessed | tf_op | source)
XLA Modules:
  0.0 166.8 jit_solution(4948075547426588957)
XLA Ops:
  0.0 0.8 convert_multiply_fusion
  0.8 1.0 copy.9
  1.9 151.3 %spread_spectra.1 = bf16[32,43,8,256]{3,2,1,0:T(8,128)(2,1)} custom-call(bf16[2,4096,512]{2,1,0:T(8,128)(2,1)} %volt.1, f32[1024,12]{1,0:T(8,128)} %bitcast.3, f32[1024,128]{1,0:T(8,128)} %constant.10.clone.low_cos, f32[1024,128]{1,0:T(8,128)} %constant.11.clone.low_sin, f32[1024,8]{1,0:T(8,128)} %constant.12.clone.high_cos, f32[1024,8]{1,0:T(8,128)} %constant.13.clone.high_sin), custom_call_target="tpu_custom_call" | custom-call | tf_op jit(solution)/shard_map/spread_spectra/pallas_call | solution.py:327
  153.2 13.6 %correlate.1 = bf16[4,1024,1024]{2,1,0:T(8,128)(2,1)} custom-call(bf16[8,4,43,8,256]{4,3,2,1,0:T(8,128)(2,1)} %bitcast.2), custom_call_target="tpu_custom_call" | custom-call | tf_op jit(solution)/shard_map/correlate/pallas_call | solution.py:357

commit v4 on v3

v4 whole, which is shorter than its diff:
```python
import functools
import math

import jax
import jax.numpy as jnp
import numpy as np
from jax import lax
from jax.experimental import pallas as pl
from jax.experimental.pallas import tpu as pltpu
from jax.sharding import PartitionSpec as P

KEEP = 512
MESH = pl.DeviceIdType.MESH


UNITS = ((0,), (1, 2), (8, 16), (9, 17), (10, 18), (3, 11), (4, 12), (5, 13), (6, 14), (7, 15))
FIRST_SUM = 2
RING = 4


def table_parts(fine, keep, owned):
    chan = (np.arange(keep) - keep // 2).reshape(-1, RING, 2, 2 * owned)
    chan = np.repeat(chan.transpose(1, 2, 0, 3).reshape(-1), 2)
    part = np.tile(np.arange(2), keep)
    low = (chan[:, None] * np.arange(128)[None, :] + part[:, None] * (fine // 4)) % fine
    high = (chan[:, None] * np.arange(0, fine, 128)[None, :]) % fine
    scale = 1.0 / math.sqrt(fine)
    step = 2.0 * np.pi / fine
    return tuple(
        x.astype(np.float32)
        for x in (np.cos(step * low) * scale, np.sin(step * low) * scale, np.cos(step * high), np.sin(step * high))
    )


def row_slots(span, history):
    slots, count = {}, 0
    for q in range(span):
        for m in range(RING + (history + span - 1 - q) // span):
            slots[q, m] = count
            count += 1
    return slots, count


class Place:
    def __init__(self):
        time, self.z_lo = lax.axis_index("tm"), lax.axis_index("inp")
        self.core, self.y = lax.rem(time, 2), lax.rem(time // 2, RING)
        self.x, self.z_hi = lax.rem(time // 8, 4), time // 32

    def device(self, y, x, z_hi, core, z_lo):
        return {"tm": ((z_hi * 4 + x) * RING + y) * 2 + core, "inp": z_lo}

    def along(self, steps):
        return self.device(lax.rem(self.y + steps + RING, RING), self.x, self.z_hi, self.core, self.z_lo)

    def flipped(self, flip):
        x_flip, z_hi_flip, core_flip, z_lo_flip = flip
        x = lax.rem(self.x // 2 + x_flip // 2, 2) * 2 + lax.rem(self.x + x_flip, 2)
        z_hi = lax.rem(self.z_hi + z_hi_flip, 2)
        core, z_lo = lax.rem(self.core + core_flip, 2), lax.rem(self.z_lo + z_lo_flip, 2)
        return self.device(self.y, x, z_hi, core, z_lo), ((core * 2 + z_hi) * 4 + x) * 2 + z_lo

    def number(self):
        return ((self.core * 2 + self.z_hi) * 4 + self.x) * 2 + self.z_lo

    def each_other(self, core, action):
        core_flip = lax.rem(self.core + core, 2)

        @pl.loop(0, 8)
        def _(outer):
            for z_lo_flip in range(2):
                flip = (lax.rem(outer, 4), outer // 4, core_flip, z_lo_flip)
                if z_lo_flip:
                    action(flip)
                else:
                    pl.when(outer + core_flip > 0)(functools.partial(action, flip))


def spread_spectra(
    frames, fine, history, volt, taps, low_cos, low_sin, high_cos, high_sin, out,
    samples, filtered, stage, heard, relay, summed, received, spectra, turning, table, wide_taps,
    in_sem, give_sem, send_sem, relay_sem, pass_sem, heard_sem, keep_sem, plane_sem, recv_sem, own_sem, out_sem,
):
    place = Place()
    core, here = place.core, place.number()
    partner = lax.axis_index("tm") + 1 - 2 * core
    span = 2 * frames
    half = samples.shape[3]
    plane = summed.shape[0]
    slots, _ = row_slots(span, history)
    order = [f for unit in UNITS for f in unit]
    slot_of = {f: i for i, f in enumerate(order)}
    barrier = pltpu.get_barrier_semaphore()

    def greet(flip):
        pl.semaphore_signal(barrier, inc=1, device_id=place.flipped(flip)[0], device_id_type=MESH)

    for which in range(2):
        place.each_other(which, greet)
    for steps in (1, -1):
        pl.semaphore_signal(barrier, inc=1, device_id=place.along(steps), device_id_type=MESH)

    def lanes(which):
        return pl.ds(pl.multiple_of(which * half, half), half)

    pieces = [(f, r) for f in range(frames) for r in range(2)]
    for f, r in pieces:
        source = volt.at[r, pl.ds(f * fine, fine), lanes(core)]
        pltpu.make_async_copy(source, samples.at[core * frames + f, r], in_sem.at[core * frames + f, r]).start()

    rows = 16

    @pl.loop(0, fine // rows)
    def _(step):
        at = pl.ds(pl.multiple_of(step * rows, rows), rows)
        tap_rows = taps[at, :].astype(jnp.float32) * (1.0 / 8192.0)
        for k in range(history + 1):
            wide_taps[k, at] = jnp.broadcast_to(tap_rows[:, k : k + 1], (rows, 128))

    pl.semaphore_wait(barrier, plane + 1)

    given = []
    for f, r in pieces:
        given.append(
            pltpu.make_async_remote_copy(
                src_ref=volt.at[r, pl.ds(f * fine, fine), lanes(1 - core)],
                dst_ref=samples.at[core * frames + f, r],
                send_sem=give_sem.at[f, r],
                recv_sem=in_sem.at[core * frames + f, r],
                device_id={"tm": partner},
                device_id_type=MESH,
            )
        )
        given[-1].start()

    @pl.loop(0, table.shape[0] // rows)
    def _(step):
        at = pl.ds(pl.multiple_of(step * rows, rows), rows)
        base_cos, base_sin = low_cos[at, :], low_sin[at, :]
        more_cos, more_sin = high_cos[at, :], high_sin[at, :]
        for block in range(fine // 128):
            turn_cos = jnp.broadcast_to(more_cos[:, block : block + 1], (rows, 128))
            turn_sin = jnp.broadcast_to(more_sin[:, block : block + 1], (rows, 128))
            table[at, pl.ds(block * 128, 128)] = (turn_cos * base_cos - turn_sin * base_sin).astype(jnp.bfloat16)
            table[at, pl.ds(fine + block * 128, 128)] = (turn_sin * base_cos + turn_cos * base_sin).astype(jnp.bfloat16)

    def remote(source, target, send, recv, device):
        pltpu.make_async_remote_copy(
            src_ref=source, dst_ref=target, send_sem=send, recv_sem=recv, device_id=device, device_id_type=MESH
        ).start()

    hops = ((0, 1), (1, -1))

    last = len(UNITS) - 1
    loads = [(unit, 0, plane) for unit in range(last)] + [(last, which * (plane // 2), plane // 2) for which in range(2)]

    def half_of(load, side):
        _, first, size = loads[load]
        return pl.ds(first + side * (size // 2), size // 2)

    def relayed(load):
        _, first, size = loads[load]
        return pl.ds(first // 2, size // 2)

    def send(load):
        unit, first, size = loads[load]
        across = lax.rem(place.y + 2, RING)
        whole = pl.ds(first, size)
        for side, steps in hops:
            remote(stage.at[at[unit], across, half_of(load, side)], relay.at[at[unit], side, relayed(load)], send_sem, relay_sem.at[load], place.along(steps))
        for side, steps in hops:
            to = lax.rem(place.y + steps + RING, RING)
            remote(stage.at[at[unit], to, whole], heard.at[at[unit], place.y, whole], send_sem, heard_sem.at[load], place.along(steps))
        pltpu.make_async_copy(stage.at[at[unit], place.y, whole], heard.at[at[unit], place.y, whole], keep_sem.at[load]).start()

    def pass_on(load):
        unit = loads[load][0]
        came_in = relay.at[at[unit], :, relayed(load)]
        pltpu.make_async_copy(came_in, came_in, relay_sem.at[load]).wait()
        for side, steps in hops:
            came = lax.rem(place.y - steps + RING, RING)
            remote(
                relay.at[at[unit], side, relayed(load)], heard.at[at[unit], came, half_of(load, side)], pass_sem, heard_sem.at[load], place.along(steps)
            )

    done = set()

    def finish(load):
        unit, first, size = loads[load]
        whole = pl.ds(first, size)
        three = heard.at[at[unit], pl.ds(0, RING - 1), whole]
        pltpu.make_async_copy(three, three, heard_sem.at[load]).wait()
        one = heard.at[at[unit], 0, whole]
        pltpu.make_async_copy(one, one, keep_sem.at[load]).wait()
        if unit < FIRST_SUM:
            return
        q = UNITS[unit][0] % span
        ms = [m for (other, m) in slots if other == q]
        parts = list(range(q, span + history, span))

        @pl.loop(first, first + size)
        def _(device):
            for m in ms:
                total = None
                for j, f in enumerate(parts):
                    if 0 <= m - j < RING:
                        term = heard[slot_of[f], m - j, device].astype(jnp.float32)
                        total = term if total is None else total + term
                summed[device, slots[q, m]] = total.astype(jnp.bfloat16)

        piece = pl.ds(slots[q, 0], len(ms))

        def spread(flip):
            device, number = place.flipped(flip)
            remote(summed.at[number, piece], received.at[here, piece], plane_sem, recv_sem.at[q], device)

        for which in range(2):
            if first <= which * (plane // 2) < first + size:
                place.each_other(which, spread)
        if first + size == plane:
            pltpu.make_async_copy(summed.at[here, piece], received.at[here, piece], own_sem.at[q]).start()

    def written(q):
        rows_of = [pl.ds(s * (span * plane) + q * plane, plane) for s in range(2)]
        return [pltpu.make_async_copy(spectra.at[:, r], out.at[:, r], out_sem.at[q, s]) for s, r in enumerate(rows_of)]

    def assemble(q):
        ms = [m for (other, m) in slots if other == q]
        piece = pl.ds(slots[q, 0], len(ms))
        others = received.at[pl.ds(0, plane - 1), piece]
        pltpu.make_async_copy(others, others, recv_sem.at[q]).wait()
        pltpu.make_async_copy(summed.at[here, piece], received.at[here, piece], own_sem.at[q]).wait()

        @pl.loop(0, 4)
        def _(group):
            group_core, group_lo = group // 2, lax.rem(group, 2)
            column = group_lo * 2 + group_core
            for lane in range(half // 128):
                cols = pl.ds(lane * 128, 128)
                for part in range(2):
                    buffer = lane * 2 + part
                    for i in range(4 * RING):
                        line, m = part * 4 + i // RING, i % RING
                        value = received[group_core * 16 + line * 2 + group_lo, slots[q, m], :, cols].astype(jnp.float32)
                        if line and (q, m + RING) in slots:
                            value = value + received[group_core * 16 + (line - 1) * 2 + group_lo, slots[q, m + RING], :, cols].astype(jnp.float32)
                        turning[buffer, pl.ds(i * 8, 8), :] = value
                    for row in range(8):
                        picked = turning[buffer, pl.ds(row, 4 * RING, stride=8), :].astype(jnp.bfloat16)
                        rows_at = pl.ds((row % 2) * (span * plane) + q * plane + part * 4 * RING, 4 * RING)
                        spectra[row // 2, rows_at, pl.ds(pl.multiple_of(column * half + lane * 128, 128), 128)] = picked
        for copy in written(q):
            copy.start()

    at = []
    begin = 0
    arrived = 0
    for unit, outputs in enumerate(UNITS):
        count = len(outputs)
        while arrived <= min(span - 1, max(outputs)):
            for r in range(2):
                pltpu.make_async_copy(samples.at[arrived, r], samples.at[arrived, r], in_sem.at[arrived, r]).wait()
            arrived += 1
        inputs = [i for i in range(span) if any(0 <= f - i <= history for f in outputs)]

        @pl.loop(0, fine // rows)
        def _(step):
            here_rows = pl.ds(pl.multiple_of(step * rows, rows), rows)
            for r in range(2):
                for lane in range(half // 128):
                    cols = pl.ds(lane * 128, 128)
                    held = {i: samples[i, r, here_rows, cols].astype(jnp.float32) for i in inputs}
                    for place_in, f in enumerate(outputs):
                        total = None
                        for i in inputs:
                            if 0 <= f - i <= history:
                                term = wide_taps[f - i, here_rows] * held[i]
                                total = term if total is None else total + term
                        filtered[place_in, pl.ds(pl.multiple_of(r * fine + step * rows, rows), rows), cols] = total.astype(jnp.bfloat16)

        @pl.loop(0, count)
        def _(f):
            product = jnp.dot(table[...], filtered[f], preferred_element_type=jnp.float32)
            stage[begin + f] = product.astype(jnp.bfloat16).reshape(stage.shape[1:])

        at.append(pl.ds(begin, count))
        begin += count
        if unit < last:
            send(unit)
        else:
            send(last)
            send(last + 1)
        if unit >= 1:
            pass_on(unit - 1)
        if unit >= 2:
            finish(unit - 2)
        if unit >= FIRST_SUM + 4:
            assemble(UNITS[unit - 4][0] % span)

    for load in (last, last + 1):
        pass_on(load)
    finish(last - 1)
    for unit in (last - 3, last - 2):
        assemble(UNITS[unit][0] % span)
    for load in (last, last + 1):
        finish(load)
    for unit in (last - 1, last):
        assemble(UNITS[unit][0] % span)
    for copy in given:
        copy.wait_send()
    sent = stage.at[:, pl.ds(0, RING - 1)]
    pltpu.make_async_copy(sent, sent, send_sem).wait()
    pltpu.make_async_copy(relay, relay, pass_sem).wait()
    others = summed.at[pl.ds(0, plane - 1)]
    pltpu.make_async_copy(others, others, plane_sem).wait()
    for q in range(span):
        for copy in written(q):
            copy.wait()


def correlate(inverse, width, spectra, out, turned_in):
    depth, total_inputs = spectra.shape[1:]
    turned_in[pl.ds(0, depth // 2), :] = -spectra[0, pl.ds(depth // 2, depth // 2), :]
    turned_in[pl.ds(depth // 2, depth // 2), :] = spectra[0, pl.ds(0, depth // 2), :]
    upper = lax.broadcasted_iota(jnp.int32, (width, width), 0) <= lax.broadcasted_iota(jnp.int32, (width, width), 1)
    contract = (((0,), (0,)), ((), ()))
    for a in range(total_inputs // width):
        rows = pl.ds(a * width, width)
        left = spectra[0, :, rows]
        real = lax.dot_general(left, spectra[0, :, pl.ds(a * width, total_inputs - a * width)], contract, preferred_element_type=jnp.float32)
        imag = lax.dot_general(left, turned_in[:, pl.ds(0, (a + 1) * width)], contract, preferred_element_type=jnp.float32)
        if a:
            out[0, rows, pl.ds(0, a * width)] = (imag[:, : a * width] * inverse).astype(jnp.bfloat16)
        middle = jnp.where(upper, real[:, :width], imag[:, a * width :])
        out[0, rows, pl.ds(a * width, width)] = (middle * inverse).astype(jnp.bfloat16)
        if (a + 1) * width < total_inputs:
            out[0, rows, pl.ds((a + 1) * width, total_inputs - (a + 1) * width)] = (real[:, width:] * inverse).astype(jnp.bfloat16)


def per_device(voltages, taps):
    history = taps.shape[0] - 1
    fine = taps.shape[1]
    frames = voltages.shape[1] // fine
    width = voltages.shape[2]
    n_time = lax.axis_size("tm")
    n_group = lax.axis_size("inp")
    devices = n_time * n_group
    chans = KEEP // devices
    half = width // 2
    span = 2 * frames
    produced = span + history
    plane = devices // RING
    rows_kept = row_slots(span, history)[1]
    tables = [jnp.asarray(x) for x in table_parts(fine, KEEP, chans)]
    vmem = pl.BlockSpec(memory_space=pltpu.VMEM)
    hbm = pl.BlockSpec(memory_space=pl.ANY)
    block = (2 * chans, half)
    biggest = max(len(unit) for unit in UNITS)
    total = width * n_group
    depth = 2 * n_time * frames
    spectra = pl.pallas_call(
        functools.partial(spread_spectra, frames, fine, history),
        out_shape=jax.ShapeDtypeStruct((chans, depth, total), jnp.bfloat16),
        in_specs=[hbm] + [vmem] * 5,
        out_specs=hbm,
        scratch_shapes=[
            pltpu.VMEM((span, 2, fine, half), jnp.bfloat16),
            pltpu.VMEM((biggest, 2 * fine, half), jnp.bfloat16),
            pltpu.VMEM((produced, RING, plane, *block), jnp.bfloat16),
            pltpu.VMEM((produced, RING, plane, *block), jnp.bfloat16),
            pltpu.VMEM((produced, 2, plane // 2, *block), jnp.bfloat16),
            pltpu.VMEM((plane, rows_kept, *block), jnp.bfloat16),
            pltpu.VMEM((plane, rows_kept, *block), jnp.bfloat16),
            pltpu.VMEM((chans, depth, total), jnp.bfloat16),
            pltpu.VMEM((4, 128, 128), jnp.float32),
            pltpu.VMEM((2 * KEEP, 2 * fine), jnp.bfloat16),
            pltpu.VMEM((history + 1, fine, 128), jnp.float32),
            pltpu.SemaphoreType.DMA((span, 2)),
            pltpu.SemaphoreType.DMA((frames, 2)),
            pltpu.SemaphoreType.DMA,
            pltpu.SemaphoreType.DMA((len(UNITS) + 1,)),
            pltpu.SemaphoreType.DMA,
            pltpu.SemaphoreType.DMA((len(UNITS) + 1,)),
            pltpu.SemaphoreType.DMA((len(UNITS) + 1,)),
            pltpu.SemaphoreType.DMA,
            pltpu.SemaphoreType.DMA((span,)),
            pltpu.SemaphoreType.DMA((span,)),
            pltpu.SemaphoreType.DMA((span, 2)),
        ],
        compiler_params=pltpu.CompilerParams(collective_id=0, has_side_effects=True, vmem_limit_bytes=62 * 2**20),
        name="spread_spectra",
    )(voltages, taps.T, *tables)
    return pl.pallas_call(
        functools.partial(correlate, 1.0 / (n_time * frames), half),
        out_shape=jax.ShapeDtypeStruct((chans, total, total), jnp.bfloat16),
        grid=(chans,),
        in_specs=[pl.BlockSpec((1, depth, total), lambda c: (c, 0, 0))],
        out_specs=pl.BlockSpec((1, total, total), lambda c: (c, 0, 0)),
        scratch_shapes=[pltpu.VMEM((depth, total), jnp.bfloat16)],
        compiler_params=pltpu.CompilerParams(vmem_limit_bytes=32 * 2**20),
        name="correlate",
    )(spectra)


def solution(mesh):
    placed = (P(None, "tm", "inp"), P())
    return jax.shard_map(
        per_device,
        mesh=mesh,
        in_specs=placed,
        out_specs=P(("tm", "inp"), None, None),
        check_vma=False,
    )
```

time: 167 us -> 162 us (0.970)
  Pallas kernels: 165 us -> 157 us
  local copies, waits for them, and re-layouts: 1.02 us -> 4.04 us
    pallas_call x1, Pallas kernels: 13.6 us -> 7.58 us  [per_device(): pl.pallas_call(functools.partial(correlate, 1.0 / (n_time * frames), half...]
    unnamed x0 -> x3, local copies, waits for them, and re-layouts: none -> 4.04 us
where the time goes in v4:
time: 162 us; the launch traced here: 161 us
  Pallas kernels  157 us (97%)
  local copies, waits for them, and re-layouts  4.04 us (2%)
    pallas_call x1, Pallas kernels, per_device(): pl.pallas_call(functools.partial(spread_spectra, frames, fine, history),...  150 us
    pallas_call x1, Pallas kernels, per_device(): pl.pallas_call(functools.partial(correlate, 1.0 / (n_time * frames), half...  7.58 us
    unnamed x3, local copies, waits for them, and re-layouts  4.04 us

profile of v4, /device:TPU:1, one launch (start us, length us, event | category | flops | bytes accessed | tf_op | source)
XLA Modules:
  0.0 161.4 jit_solution(12914073326497296997)
XLA Ops:
  0.0 1.9 %copy.7 = s32[12,1024]{0,1:T(8,128)} copy(s32[12,1024]{1,0:T(8,128)} %param.7) | data formatting | bytes 98304 | tf_op args[1]
  1.9 149.7 %spread_spectra.1.spectra = bf16[4,512,1024]{2,1,0:T(8,128)(2,1)} custom-call(bf16[2,4096,512]{2,1,0:T(8,128)(2,1)} %volt.1, s32[1024,12]{1,0:T(8,128)} %bitcast.1, f32[1024,128]{1,0:T(8,128)} %constant.8.clone.low_cos, f32[1024,128]{1,0:T(8,128)} %constant.9.clone.low_sin, f32[1024,8]{1,0:T(8,128)} %constant.10.clone.high_cos, ...), custom_call_target="tpu_custom_call" | custom-call | tf_op jit(solution)/shard_map/spread_spectra/pallas_call | solution.py:361
  151.6 0.0 copy-start
  151.6 2.2 %copy-done = bf16[4,512,1024]{2,1,0:T(8,128)(2,1)S(1)} copy-done((bf16[4,512,1024]{2,1,0:T(8,128)(2,1)S(1)}, bf16[4,512,1024]{2,1,0:T(8,128)(2,1)}, u32[]{:S(2)}) %copy-start) | copy-done | bytes 4194328
  153.8 7.6 %correlate.1 = bf16[4,1024,1024]{2,1,0:T(8,128)(2,1)} custom-call(bf16[4,512,1024]{2,1,0:T(8,128)(2,1)S(1)} %copy-done), custom_call_target="tpu_custom_call" | custom-call | tf_op jit(solution)/shard_map/correlate/pallas_call | solution.py:393
Async XLA Ops:
  151.6 2.2 %copy-start = (bf16[4,512,1024]{2,1,0:T(8,128)(2,1)S(1)}, bf16[4,512,1024]{2,1,0:T(8,128)(2,1)}, u32[]{:S(2)}) copy-start(bf16[4,512,1024]{2,1,0:T(8,128)(2,1)} %spread_spectra.1.spectra) | copy-start | bytes 12582916

commit v5 on v4

--- a/solution.py
+++ b/solution.py
@@ -23,12 +23,12 @@
     chan = np.repeat(chan.transpose(1, 2, 0, 3).reshape(-1), 2)
     part = np.tile(np.arange(2), keep)
     low = (chan[:, None] * np.arange(128)[None, :] + part[:, None] * (fine // 4)) % fine
-    high = (chan[:, None] * np.arange(0, fine, 128)[None, :]) % fine
+    turn = np.broadcast_to(((chan * 128) % fine)[:16, None], (16, 128))
+    assert np.array_equal((chan * 128) % fine, np.tile(turn[:, 0], len(chan) // 16))
     scale = 1.0 / math.sqrt(fine)
     step = 2.0 * np.pi / fine
     return tuple(
-        x.astype(np.float32)
-        for x in (np.cos(step * low) * scale, np.sin(step * low) * scale, np.cos(step * high), np.sin(step * high))
+        x.astype(np.float32) for x in (np.cos(step * low) * scale, np.sin(step * low) * scale, np.cos(step * turn), np.sin(step * turn))
     )
 
 
@@ -69,15 +69,15 @@
         @pl.loop(0, 8)
         def _(outer):
             for z_lo_flip in range(2):
-                flip = (lax.rem(outer, 4), outer // 4, core_flip, z_lo_flip)
+                flip = (lax.rem(outer + 2, 4), 1 - outer // 4, core_flip, z_lo_flip)
                 if z_lo_flip:
                     action(flip)
                 else:
-                    pl.when(outer + core_flip > 0)(functools.partial(action, flip))
+                    pl.when(flip[0] + flip[1] + core_flip > 0)(functools.partial(action, flip))
 
 
 def spread_spectra(
-    frames, fine, history, volt, taps, low_cos, low_sin, high_cos, high_sin, out,
+    frames, fine, history, volt, taps, low_cos, low_sin, turn_cos, turn_sin, out,
     samples, filtered, stage, heard, relay, summed, received, spectra, turning, table, wide_taps,
     in_sem, give_sem, send_sem, relay_sem, pass_sem, heard_sem, keep_sem, plane_sem, recv_sem, own_sem, out_sem,
 ):
@@ -110,12 +110,24 @@
 
     rows = 16
 
-    @pl.loop(0, fine // rows)
+    @pl.loop(0, table.shape[0] // rows)
     def _(step):
         at = pl.ds(pl.multiple_of(step * rows, rows), rows)
-        tap_rows = taps[at, :].astype(jnp.float32) * (1.0 / 8192.0)
-        for k in range(history + 1):
-            wide_taps[k, at] = jnp.broadcast_to(tap_rows[:, k : k + 1], (rows, 128))
+        now_cos, now_sin = low_cos[at, :], low_sin[at, :]
+        by_cos, by_sin = turn_cos[...], turn_sin[...]
+        for block in range(fine // 128):
+            table[at, pl.ds(block * 128, 128)] = now_cos.astype(jnp.bfloat16)
+            table[at, pl.ds(fine + block * 128, 128)] = now_sin.astype(jnp.bfloat16)
+            now_cos, now_sin = now_cos * by_cos - now_sin * by_sin, now_sin * by_cos + now_cos * by_sin
+
+    whole = taps[...].astype(jnp.float32).astype(jnp.bfloat16)
+    tap_of = lax.broadcasted_iota(jnp.int32, (history + 1, 256), 0)
+    lane_half = lax.broadcasted_iota(jnp.int32, (history + 1, 256), 1) // 128
+    for k in range(0, history + 1, 2):
+        pick = jnp.where(tap_of == k + lane_half, 1.0, 0.0).astype(jnp.bfloat16)
+        wide = lax.dot_general(whole, pick, (((0,), (0,)), ((), ())), preferred_element_type=jnp.float32) * (1.0 / 8192.0)
+        wide_taps[k] = wide[:, :128]
+        wide_taps[k + 1] = wide[:, 128:]
 
     pl.semaphore_wait(barrier, plane + 1)
 
@@ -133,17 +145,6 @@
         )
         given[-1].start()
 
-    @pl.loop(0, table.shape[0] // rows)
-    def _(step):
-        at = pl.ds(pl.multiple_of(step * rows, rows), rows)
-        base_cos, base_sin = low_cos[at, :], low_sin[at, :]
-        more_cos, more_sin = high_cos[at, :], high_sin[at, :]
-        for block in range(fine // 128):
-            turn_cos = jnp.broadcast_to(more_cos[:, block : block + 1], (rows, 128))
-            turn_sin = jnp.broadcast_to(more_sin[:, block : block + 1], (rows, 128))
-            table[at, pl.ds(block * 128, 128)] = (turn_cos * base_cos - turn_sin * base_sin).astype(jnp.bfloat16)
-            table[at, pl.ds(fine + block * 128, 128)] = (turn_sin * base_cos + turn_cos * base_sin).astype(jnp.bfloat16)
-
     def remote(source, target, send, recv, device):
         pltpu.make_async_remote_copy(
             src_ref=source, dst_ref=target, send_sem=send, recv_sem=recv, device_id=device, device_id_type=MESH
@@ -162,12 +163,15 @@
         _, first, size = loads[load]
         return pl.ds(first // 2, size // 2)
 
-    def send(load):
-        unit, first, size = loads[load]
+    def send_far(load):
+        unit = loads[load][0]
         across = lax.rem(place.y + 2, RING)
-        whole = pl.ds(first, size)
         for side, steps in hops:
             remote(stage.at[at[unit], across, half_of(load, side)], relay.at[at[unit], side, relayed(load)], send_sem, relay_sem.at[load], place.along(steps))
+
+    def send_near(load):
+        unit, first, size = loads[load]
+        whole = pl.ds(first, size)
         for side, steps in hops:
             to = lax.rem(place.y + steps + RING, RING)
             remote(stage.at[at[unit], to, whole], heard.at[at[unit], place.y, whole], send_sem, heard_sem.at[load], place.along(steps))
@@ -285,25 +289,25 @@
 
         at.append(pl.ds(begin, count))
         begin += count
-        if unit < last:
-            send(unit)
-        else:
-            send(last)
-            send(last + 1)
         if unit >= 1:
             pass_on(unit - 1)
+        send_far(unit)
+        if unit == last:
+            send_far(last + 1)
+        send_near(unit)
         if unit >= 2:
             finish(unit - 2)
         if unit >= FIRST_SUM + 4:
             assemble(UNITS[unit - 4][0] % span)
 
-    for load in (last, last + 1):
-        pass_on(load)
     finish(last - 1)
-    for unit in (last - 3, last - 2):
-        assemble(UNITS[unit][0] % span)
-    for load in (last, last + 1):
-        finish(load)
+    pass_on(last)
+    send_near(last + 1)
+    pass_on(last + 1)
+    assemble(UNITS[last - 3][0] % span)
+    finish(last)
+    assemble(UNITS[last - 2][0] % span)
+    finish(last + 1)
     for unit in (last - 1, last):
         assemble(UNITS[unit][0] % span)
     for copy in given:
@@ -389,7 +393,7 @@
         ],
         compiler_params=pltpu.CompilerParams(collective_id=0, has_side_effects=True, vmem_limit_bytes=62 * 2**20),
         name="spread_spectra",
-    )(voltages, taps.T, *tables)
+    )(voltages, taps, *tables)
     return pl.pallas_call(
         functools.partial(correlate, 1.0 / (n_time * frames), half),
         out_shape=jax.ShapeDtypeStruct((chans, total, total), jnp.bfloat16),
@@ -397,7 +401,7 @@
         in_specs=[pl.BlockSpec((1, depth, total), lambda c: (c, 0, 0))],
         out_specs=pl.BlockSpec((1, total, total), lambda c: (c, 0, 0)),
         scratch_shapes=[pltpu.VMEM((depth, total), jnp.bfloat16)],
-        compiler_params=pltpu.CompilerParams(vmem_limit_bytes=32 * 2**20),
+        compiler_params=pltpu.CompilerParams(vmem_limit_bytes=62 * 2**20),
         name="correlate",
     )(spectra)
 

time: 162 us -> 140 us (0.86)
  Pallas kernels: 157 us -> 140 us
  local copies, waits for them, and re-layouts: 4.04 us -> 0 us
    pallas_call x1, Pallas kernels: 150 us -> 131 us  [per_device(): pl.pallas_call(functools.partial(spread_spectra, frames, fine, history),...]
    unnamed x3 -> x0, local copies, waits for them, and re-layouts: 4.04 us -> none
    pallas_call x1, Pallas kernels: 7.58 us -> 9.3 us  [per_device(): pl.pallas_call(functools.partial(correlate, 1.0 / (n_time * frames), half...]
where the time goes in v5:
time: 140 us
  Pallas kernels  140 us (100%)
    pallas_call x1, Pallas kernels, per_device(): pl.pallas_call(functools.partial(spread_spectra, frames, fine, history),...  131 us
    pallas_call x1, Pallas kernels, per_device(): pl.pallas_call(functools.partial(correlate, 1.0 / (n_time * frames), half...  9.3 us

profile of v5, /device:TPU:1, one launch (start us, length us, event | category | flops | bytes accessed | tf_op | source)
XLA Modules:
  0.0 140.2 jit_solution(1229178293366949131)
XLA Ops:
  0.0 130.9 %spread_spectra.1.spectra = bf16[4,512,1024]{2,1,0:T(8,128)(2,1)} custom-call(bf16[2,4096,512]{2,1,0:T(8,128)(2,1)} %volt.1, s32[12,1024]{1,0:T(8,128)} %taps.1, f32[1024,128]{1,0:T(8,128)} %constant.8.clone.low_cos, f32[1024,128]{1,0:T(8,128)} %constant.9.clone.low_sin, f32[16,128]{1,0:T(8,128)} %constant.10.clone.turn_cos, f32[16,128]{1,0:T(8,128)} %constant.11.clone.turn_sin), custom_call_target="tpu_custom_call" | custom-call | tf_op jit(solution)/shard_map/spread_spectra/pallas_call | solution.py:365
  130.9 9.3 %correlate.1 = bf16[4,1024,1024]{2,1,0:T(8,128)(2,1)} custom-call(bf16[4,512,1024]{2,1,0:T(8,128)(2,1)} %spread_spectra.1.spectra), custom_call_target="tpu_custom_call" | custom-call | tf_op jit(solution)/shard_map/correlate/pallas_call | solution.py:397

commit v6 on v5

--- a/solution.py
+++ b/solution.py
@@ -13,7 +13,7 @@
 MESH = pl.DeviceIdType.MESH
 
 
-UNITS = ((0,), (1, 2), (8, 16), (9, 17), (10, 18), (3, 11), (4, 12), (5, 13), (6, 14), (7, 15))
+UNITS = ((0,), (1,), (8, 16), (9, 17), (2, 10, 18), (3, 11), (4, 12), (5, 13), (6, 14), (7, 15))
 FIRST_SUM = 2
 RING = 4
 

time: 140 us -> 140 us (level)
  no operation moved by 1% of the time
where the time goes in v6:
time: 140 us
  Pallas kernels  140 us (100%)
    pallas_call x1, Pallas kernels, per_device(): pl.pallas_call(functools.partial(spread_spectra, frames, fine, history),...  131 us
    pallas_call x1, Pallas kernels, per_device(): pl.pallas_call(functools.partial(correlate, 1.0 / (n_time * frames), half...  9.3 us

profile of v6, /device:TPU:1, one launch (start us, length us, event | category | flops | bytes accessed | tf_op | source)
XLA Modules:
  0.0 139.9 jit_solution(18399920267298856083)
XLA Ops:
  0.0 130.6 %spread_spectra.1.spectra = bf16[4,512,1024]{2,1,0:T(8,128)(2,1)} custom-call(bf16[2,4096,512]{2,1,0:T(8,128)(2,1)} %volt.1, s32[12,1024]{1,0:T(8,128)} %taps.1, f32[1024,128]{1,0:T(8,128)} %constant.8.clone.low_cos, f32[1024,128]{1,0:T(8,128)} %constant.9.clone.low_sin, f32[16,128]{1,0:T(8,128)} %constant.10.clone.turn_cos, f32[16,128]{1,0:T(8,128)} %constant.11.clone.turn_sin), custom_call_target="tpu_custom_call" | custom-call | tf_op jit(solution)/shard_map/spread_spectra/pallas_call | solution.py:365
  130.6 9.3 %correlate.1 = bf16[4,1024,1024]{2,1,0:T(8,128)(2,1)} custom-call(bf16[4,512,1024]{2,1,0:T(8,128)(2,1)} %spread_spectra.1.spectra), custom_call_target="tpu_custom_call" | custom-call | tf_op jit(solution)/shard_map/correlate/pallas_call | solution.py:397
